TPU v7x, 1024 devices: a whole 4x8x16 slice. The times are simulated.
1024 devices in a mesh: dp: 16 (over z), section: 8 (over x, core), expert: 8 (over y).
Axes of the slice: x: 4, y: 8, z: 16, core: 2. Of those that a mesh axis runs over, the one named last changes fastest.
Arguments:
- act_in: bfloat16 [8, 8192, 2048], P('section', ('dp', 'expert')), may hold values from -6 to 6
- saved_in: bfloat16 [8, 8192, 2048], P('section', ('dp', 'expert')), may hold values from -6 to 6
- grad_in: bfloat16 [8, 8192, 2048], P('section', ('dp', 'expert')), may hold values from -6 to 6
- fwd_ids: int32 [8, 8192, 2], P('section', ('dp', 'expert')), may hold values from 0 to 7, all different within a row; in each aligned block of 64 rows (0 to 63, 64 to 127, ..., all dimensions but the last counted through in order) at most 20 rows name the same one
- bwd_ids: int32 [8, 8192, 2], P('section', ('dp', 'expert')), may hold values from 0 to 7, all different within a row; in each aligned block of 64 rows (0 to 63, 64 to 127, ..., all dimensions but the last counted through in order) at most 20 rows name the same one
- fwd_gates: float32 [8, 8192, 2], P('section', ('dp', 'expert')), may hold values from 0.2 to 1
- bwd_gates: float32 [8, 8192, 2], P('section', ('dp', 'expert')), may hold values from 0.2 to 1
- norm_gain: float32 [8, 2048], P('section'), may hold values from 0.5 to 1.5
- w_gate: bfloat16 [8, 8, 2048, 384], P('section', 'expert'), may hold values from -0.125 to 0.125
- w_up: bfloat16 [8, 8, 2048, 384], P('section', 'expert'), may hold values from -0.125 to 0.125
- w_down: bfloat16 [8, 8, 384, 2048], P('section', 'expert'), may hold values from -0.3125 to 0.3125
Outputs:
- act_out: bfloat16 [8, 8192, 2048], P('section', ('dp', 'expert'))
- grad_out: bfloat16 [8, 8192, 2048], P('section', ('dp', 'expert'))
- weight_grads: float32 [8, 8, 2048, 1152], P('section', 'expert', 'dp')
Inputs may be any that keep to these rules, and one draw needn't show every extreme that they name: `fwd_ids`: the 2 entries of a token name different experts. In each aligned block of 64 tokens of a section (the tokens of one device), no expert is named by more than 20 entries, and in every draw some block has an expert named exactly 20 times. `bwd_ids`: the 2 entries of a token name different experts. In each aligned block of 64 tokens of a section (the tokens of one device), no expert is named by more than 20 entries, and in every draw some block has an expert named exactly 20 times.
All inputs are finite; a program needn't handle non-finite values.
Results may differ from a plain program's by a relative error of at most 0.017.
Values may be sent and summed in bfloat16 or wider, within the bound.
No kernel may reach another device: no remote copies, remote signals or barrier semaphores. Data moves between devices by JAX's collectives and lax.ppermute only.
A program may use at most 64 MiB of HBM per device.

v0:
```python
import jax
import jax.numpy as jnp
from jax import lax
from jax.sharding import PartitionSpec as P

EPS = 1e-06


def padded(block, sides, width):
    for axis, dim in sides:
        count = lax.axis_size(axis)
        forward = [(i, i + 1) for i in range(count - 1)]
        forward.append((count - 1, 0))
        backward = [(target, source) for source, target in forward]
        low = lax.ppermute(
            lax.slice_in_dim(block, block.shape[dim] - width, None, axis=dim), axis, forward
        )
        high = lax.ppermute(lax.slice_in_dim(block, 0, width, axis=dim), axis, backward)
        block = jnp.concatenate([low, block, high], axis=dim)
    return block


def rms_norm(rows, gain):
    wide = rows.astype(jnp.float32)
    factor = lax.rsqrt(jnp.mean(wide * wide, axis=-1, keepdims=True) + EPS)
    return wide * factor * gain


def place_rows(ids, experts, capacity):
    flat = ids.reshape(-1)
    onehot = (flat[:, None] == jnp.arange(experts, dtype=jnp.int32)[None, :]).astype(jnp.int32)
    before = jnp.cumsum(onehot, axis=0) - onehot
    slot = jnp.sum(before * onehot, axis=1)
    return flat * capacity + slot


def place_matrix(dest, experts, capacity):
    return (jnp.arange(experts * capacity, dtype=jnp.int32)[:, None] == dest[None, :]).astype(
        jnp.bfloat16
    )


def shards(
    act_in,
    saved_in,
    grad_in,
    fwd_ids,
    bwd_ids,
    fwd_gates,
    bwd_gates,
    norm_gain,
    w_gate,
    w_up,
    w_down,
):
    experts = lax.axis_size("expert")
    replicas = lax.axis_size("dp")
    tokens = act_in.shape[1]
    width = act_in.shape[2]
    topk = fwd_ids.shape[2]
    capacity = min(tokens, 5 * tokens * topk // (4 * experts))
    gain = norm_gain[0]
    weight_gate = w_gate[0, 0]
    weight_up = w_up[0, 0]
    weight_down = w_down[0, 0]
    here = act_in[0]
    upstream = grad_in[0].astype(jnp.float32)
    normed_fwd = rms_norm(here, gain).astype(jnp.bfloat16)
    normed_wide, pull_back = jax.vjp(lambda v: rms_norm(v, gain), saved_in[0].astype(jnp.float32))
    normed_bwd = normed_wide.astype(jnp.bfloat16)
    out_grad = (
        (bwd_gates[0][:, :, None] * upstream[:, None, :])
        .astype(jnp.bfloat16)
        .reshape(tokens * topk, width)
    )
    dest_fwd = place_rows(fwd_ids[0], experts, capacity)
    dest_bwd = place_rows(bwd_ids[0], experts, capacity)
    send_fwd = jnp.dot(
        place_matrix(dest_fwd, experts, capacity),
        jnp.repeat(normed_fwd, topk, axis=0),
        preferred_element_type=jnp.float32,
    ).astype(jnp.bfloat16)
    joined = jnp.concatenate([jnp.repeat(normed_bwd, topk, axis=0), out_grad], axis=1)
    send_joined = jnp.dot(
        place_matrix(dest_bwd, experts, capacity), joined, preferred_element_type=jnp.float32
    ).astype(jnp.bfloat16)
    send_bwd = send_joined[:, :width].reshape(experts, capacity, width)
    send_grad = send_joined[:, width:].reshape(experts, capacity, width)
    recv_fwd, recv_bwd, recv_grad = (
        lax.all_to_all(
            send_fwd.reshape(experts, capacity, width),
            "expert",
            split_axis=0,
            concat_axis=0,
            tiled=True,
        ),
        lax.all_to_all(send_bwd, "expert", split_axis=0, concat_axis=0, tiled=True),
        lax.all_to_all(send_grad, "expert", split_axis=0, concat_axis=0, tiled=True),
    )
    rows_fwd = recv_fwd.reshape(-1, width)
    rows_bwd = recv_bwd.reshape(-1, width)
    rows_grad = recv_grad.reshape(-1, width)
    pre_gate = jnp.dot(rows_fwd, weight_gate, preferred_element_type=jnp.float32)
    pre_up = jnp.dot(rows_fwd, weight_up, preferred_element_type=jnp.float32)
    hidden_fwd = (jax.nn.silu(pre_gate) * pre_up).astype(jnp.bfloat16)
    out_fwd = jnp.dot(hidden_fwd, weight_down, preferred_element_type=jnp.float32).astype(
        jnp.bfloat16
    )
    contract_last = (((1,), (1,)), ((), ()))
    back_gate = jnp.dot(rows_bwd, weight_gate, preferred_element_type=jnp.float32)
    back_up = jnp.dot(rows_bwd, weight_up, preferred_element_type=jnp.float32)
    sig = jax.nn.sigmoid(back_gate)
    silu_gate = jax.nn.silu(back_gate)
    hidden_bwd = (silu_gate * back_up).astype(jnp.bfloat16)
    hidden_grad = lax.dot_general(
        rows_grad, weight_down, contract_last, preferred_element_type=jnp.float32
    )
    gate_grad = (hidden_grad * back_up * sig * (1.0 + back_gate * (1.0 - sig))).astype(jnp.bfloat16)
    up_grad = (hidden_grad * silu_gate).astype(jnp.bfloat16)
    slot_grad = (
        lax.dot_general(gate_grad, weight_gate, contract_last, preferred_element_type=jnp.float32)
        + lax.dot_general(up_grad, weight_up, contract_last, preferred_element_type=jnp.float32)
    ).astype(jnp.bfloat16)
    back_fwd, back_grad = (
        lax.all_to_all(
            out_fwd.reshape(experts, capacity, width),
            "expert",
            split_axis=0,
            concat_axis=0,
            tiled=True,
        ),
        lax.all_to_all(
            slot_grad.reshape(experts, capacity, width),
            "expert",
            split_axis=0,
            concat_axis=0,
            tiled=True,
        ),
    )
    picked = back_fwd.reshape(-1, width)[dest_fwd].reshape(tokens, topk, width).astype(jnp.float32)
    layer_out = (
        here.astype(jnp.float32) + jnp.sum(fwd_gates[0][:, :, None] * picked, axis=1)
    ).astype(jnp.bfloat16)
    normed_grad = jnp.sum(
        back_grad.reshape(-1, width)[dest_bwd].reshape(tokens, topk, width).astype(jnp.float32),
        axis=1,
    )
    input_grad = (upstream + pull_back(normed_grad)[0]).astype(jnp.bfloat16)
    passed = padded(jnp.stack([input_grad, layer_out]), (("section", 0),), 1)
    act_out = passed[0][None]
    grad_out = passed[3][None]
    scale = 1.0 / replicas
    contract_first = (((0,), (0,)), ((), ()))
    slot_rows = rows_bwd.shape[0]
    hid = hidden_bwd.shape[1]
    upper_right = jnp.concatenate(
        [gate_grad, up_grad, jnp.zeros((slot_rows, hid), jnp.bfloat16)], axis=1
    )
    lower_right = jnp.concatenate(
        [jnp.zeros((slot_rows, 2 * hid), jnp.bfloat16), hidden_bwd], axis=1
    )
    right_blocks = jnp.concatenate([upper_right, lower_right], axis=0)
    left_rows = jnp.concatenate([rows_bwd, rows_grad], axis=0)
    summed = lax.psum_scatter(
        (
            lax.dot_general(
                left_rows, right_blocks, contract_first, preferred_element_type=jnp.float32
            )
            * scale
        ).astype(jnp.bfloat16),
        "dp",
        scatter_dimension=0,
        tiled=True,
    ).astype(jnp.float32)
    return (act_out, grad_out, summed[None, None])


def solution(mesh):
    in_specs = (
        P("section", ("dp", "expert"), None),
        P("section", ("dp", "expert"), None),
        P("section", ("dp", "expert"), None),
        P("section", ("dp", "expert"), None),
        P("section", ("dp", "expert"), None),
        P("section", ("dp", "expert"), None),
        P("section", ("dp", "expert"), None),
        P("section", None),
        P("section", "expert", None, None),
        P("section", "expert", None, None),
        P("section", "expert", None, None),
    )
    out_specs = (
        P("section", ("dp", "expert"), None),
        P("section", ("dp", "expert"), None),
        P("section", "expert", "dp", None),
    )
    return jax.shard_map(shards, mesh=mesh, in_specs=in_specs, out_specs=out_specs, check_vma=False)
```

profile of v0, /device:TPU:448, one launch (start us, length us, event | category | flops | bytes accessed | tf_op | source)
XLA Modules:
  0.0 206.0 jit_solution(9107904488213092142)
XLA Ops:
  13.1 1.9 mul.223
  17.0 7.1 %all-to-all-start.3 = ((bf16[8,20,2048]{2,1,0:T(8,128)(2,1)}), bf16[8,20,2048]{2,1,0:T(8,128)(2,1)}, u32[]{:S(2)}, u32[]{:S(2)}) async-start(bf16[8,20,2048]{2,1,0:T(8,128)(2,1)} %reshape.229), calls=%async_computation.3 | async-start | bytes 1572864 | tf_op jit(solution)/shard_map/all_to_all | solution.py:97
  25.1 22.2 %all-to-all-done.3 = bf16[8,20,2048]{2,1,0:T(8,128)(2,1)} async-done(((bf16[8,20,2048]{2,1,0:T(8,128)(2,1)}), bf16[8,20,2048]{2,1,0:T(8,128)(2,1)}, u32[]{:S(2)}, u32[]{:S(2)}) %all-to-all-start.3) | async-done | bytes 655392 | tf_op jit(solution)/shard_map/all_to_all | solution.py:97
  47.3 4.2 %all-to-all-start.2 = ((bf16[8,20,2048]{2,1,0:T(8,128)(2,1)}), bf16[8,20,2048]{2,1,0:T(8,128)(2,1)}, u32[]{:S(2)}, u32[]{:S(2)}) async-start(bf16[8,20,2048]{2,1,0:T(8,128)(2,1)} %reshape.227), calls=%async_computation.2 | async-start | bytes 1572864 | tf_op jit(solution)/shard_map/all_to_all | solution.py:98
  51.6 2.0 reshape.230
  53.6 1.6 fusion.12
  55.2 19.9 %all-to-all-done.2 = bf16[8,20,2048]{2,1,0:T(8,128)(2,1)} async-done(((bf16[8,20,2048]{2,1,0:T(8,128)(2,1)}), bf16[8,20,2048]{2,1,0:T(8,128)(2,1)}, u32[]{:S(2)}, u32[]{:S(2)}) %all-to-all-start.2) | async-done | bytes 655392 | tf_op jit(solution)/shard_map/all_to_all | solution.py:98
  75.1 2.0 reshape.228
  77.1 2.3 %fusion.2 = f32[160,384]{1,0:T(8,128)S(1)} fusion(bf16[160,2048]{1,0:T(8,128)(2,1)} %reshape.228, bf16[1,1,384,2048]{3,2,1,0:T(8,128)(2,1)} %param.21), kind=kOutput, calls=%fused_computation.9 | convolution fusion | flops 251658240 | bytes 2473984 | tf_op jit(solution)/shard_map/dot_general | solution.py:115
  80.7 4.0 %fusion = bf16[2048,1152]{1,0:T(8,128)(2,1)} fusion(bf16[160,2048]{1,0:T(8,128)(2,1)S(1)} %copy-done.7, bf16[160,2048]{1,0:T(8,128)(2,1)S(1)} %copy-done.6, bf16[160,384]{1,0:T(8,128)(2,1)S(1)} %get-tuple-element.5, bf16[160,384]{1,0:T(8,128)(2,1)S(1)} %broadcast_in_dim.16, bf16[160,384]{1,0:T(8,128)(2,1)S(1)} %get-tuple-element.7, ...), kind=kOutput, calls=%fused_computation.3 | convolution fusion | flops 1520975872 | bytes 6520832 | tf_op jit(solution)/shard_map/dot_general | solution.py:166
  88.3 3.7 %all-to-all-start.4 = ((bf16[8,20,2048]{2,1,0:T(8,128)(2,1)}), bf16[8,20,2048]{2,1,0:T(8,128)(2,1)S(1)}, u32[]{:S(2)}, u32[]{:S(2)}) async-start(bf16[8,20,2048]{2,1,0:T(8,128)(2,1)} %reshape.231), calls=%async_computation.4 | async-start | bytes 1572864 | tf_op jit(solution)/shard_map/all_to_all | solution.py:132
  93.2 20.3 %all-to-all-done.4 = bf16[8,20,2048]{2,1,0:T(8,128)(2,1)S(1)} async-done(((bf16[8,20,2048]{2,1,0:T(8,128)(2,1)}), bf16[8,20,2048]{2,1,0:T(8,128)(2,1)S(1)}, u32[]{:S(2)}, u32[]{:S(2)}) %all-to-all-start.4) | async-done | bytes 655392 | tf_op jit(solution)/shard_map/all_to_all | solution.py:132
  116.6 1.9 fusion.53
  121.1 27.9 %all_to_all.25 = bf16[8,20,2048]{2,1,0:T(8,128)(2,1)} all-to-all(bf16[8,20,2048]{2,1,0:T(8,128)(2,1)} %reshape.222), channel_id=1, replica_groups=mesh['dp'=16,'section'=8,'expert'=8] {'expert'}, dimensions={0} | all-to-all | bytes 1310720 | tf_op jit(solution)/shard_map/all_to_all | solution.py:90
  148.9 2.0 reshape.223
  151.0 2.3 %fusion.14 = f32[160,384]{1,0:T(8,128)} fusion(bf16[160,2048]{1,0:T(8,128)(2,1)} %reshape.223, bf16[1,1,2048,384]{3,2,1,0:T(8,128)(2,1)S(1)} %copy-done.2), kind=kOutput, calls=%fused_computation.21 | convolution fusion | flops 251658240 | bytes 2473984 | tf_op jit(solution)/shard_map/dot_general | solution.py:103
  153.3 2.7 %convolution_convert_fusion.1 = bf16[160,2048]{1,0:T(8,128)(2,1)S(1)} fusion(bf16[1,1,384,2048]{3,2,1,0:T(8,128)(2,1)} %param.21, bf16[160,2048]{1,0:T(8,128)(2,1)} %reshape.223, bf16[1,1,2048,384]{3,2,1,0:T(8,128)(2,1)S(1)} %copy-done, f32[160,384]{1,0:T(8,128)} %fusion.14), kind=kOutput, calls=%fused_computation.7 | convolution fusion | flops 504012800 | bytes 4702208 | tf_op jit(solution)/shard_map/dot_general | solution.py:106
  157.1 3.5 %all-to-all-start.1 = ((bf16[8,20,2048]{2,1,0:T(8,128)(2,1)}), bf16[8,20,2048]{2,1,0:T(8,128)(2,1)S(1)}, u32[]{:S(2)}, u32[]{:S(2)}) async-start(bf16[8,20,2048]{2,1,0:T(8,128)(2,1)} %reshape.224), calls=%async_computation.1 | async-start | bytes 1572864 | tf_op jit(solution)/shard_map/all_to_all | solution.py:125
  162.6 1.9 collective-permute-start.1
  164.5 19.2 %all-to-all-done.1 = bf16[8,20,2048]{2,1,0:T(8,128)(2,1)S(1)} async-done(((bf16[8,20,2048]{2,1,0:T(8,128)(2,1)}), bf16[8,20,2048]{2,1,0:T(8,128)(2,1)S(1)}, u32[]{:S(2)}, u32[]{:S(2)}) %all-to-all-start.1) | async-done | bytes 655392 | tf_op jit(solution)/shard_map/all_to_all | solution.py:125
  183.8 1.7 gather_fusion
  185.5 1.7 reshape.234
  188.9 7.0 %collective-permute-done = bf16[1,64,2048]{2,1,0:T(8,128)(2,1)S(1)} collective-permute-done((bf16[1,64,2048]{2,1,0:T(8,128)(2,1)S(1)}, bf16[1,64,2048]{2,1,0:T(8,128)(2,1)S(1)}, u32[]{:S(2)}, u32[]{:S(2)}) %collective-permute-start) | collective-permute-done | bytes 262176 | tf_op jit(solution)/shard_map/ppermute | solution.py:15
  195.9 1.8 bitcast_convert_fusion
  (115 shorter events, 26.3 us)
Async XLA Ops:
  7.2 72.3 %copy-start = (bf16[1,1,2048,384]{3,2,1,0:T(8,128)(2,1)S(1)}, bf16[1,1,2048,384]{3,2,1,0:T(8,128)(2,1)}, u32[]{:S(2)}) copy-start(bf16[1,1,2048,384]{3,2,1,0:T(8,128)(2,1)} %param.20) | copy-start | bytes 4718596
  7.2 4.3 %copy-start.10 = (bf16[1,64,2048]{2,1,0:T(8,128)(2,1)S(1)}, bf16[1,64,2048]{2,1,0:T(8,128)(2,1)}, u32[]{:S(2)}) copy-start(bf16[1,64,2048]{2,1,0:T(8,128)(2,1)} %param.13) | copy-start | bytes 786436
  11.5 3.5 %copy-start.18 = (f32[1,64,2]{1,2,0:T(2,128)S(1)}, f32[1,64,2]{1,2,0:T(2,128)}, u32[]{:S(2)}) copy-start(f32[1,64,2]{1,2,0:T(2,128)} %param.17) | copy-start | bytes 1540
  17.0 30.3 %all-to-all-start.3 = ((bf16[8,20,2048]{2,1,0:T(8,128)(2,1)}), bf16[8,20,2048]{2,1,0:T(8,128)(2,1)}, u32[]{:S(2)}, u32[]{:S(2)}) async-start(bf16[8,20,2048]{2,1,0:T(8,128)(2,1)} %reshape.229), calls=%async_computation.3 | async-start | bytes 1572864 | tf_op jit(solution)/shard_map/all_to_all | solution.py:97
  25.1 28.5 %copy-start.1 = (bf16[1,1,2048,384]{3,2,1,0:T(8,128)(2,1)S(1)}, bf16[1,1,2048,384]{3,2,1,0:T(8,128)(2,1)}, u32[]{:S(2)}) copy-start(bf16[1,1,2048,384]{3,2,1,0:T(8,128)(2,1)} %param.19) | copy-start | bytes 4718596
  47.3 27.8 %all-to-all-start.2 = ((bf16[8,20,2048]{2,1,0:T(8,128)(2,1)}), bf16[8,20,2048]{2,1,0:T(8,128)(2,1)}, u32[]{:S(2)}, u32[]{:S(2)}) async-start(bf16[8,20,2048]{2,1,0:T(8,128)(2,1)} %reshape.227), calls=%async_computation.2 | async-start | bytes 1572864 | tf_op jit(solution)/shard_map/all_to_all | solution.py:98
  51.6 144.4 %reduce-scatter.2.cloned.1.call-start = ((), (), s32[]{:S(2)}) async-start(), calls=%async_computation.6 | async-start | bytes 5013504 | tf_op jit(solution)/shard_map/reduce_scatter | solution.py:164
  77.1 2.3 %copy-start.6 = (bf16[160,2048]{1,0:T(8,128)(2,1)S(1)}, bf16[160,2048]{1,0:T(8,128)(2,1)}, u32[]{:S(2)}) copy-start(bf16[160,2048]{1,0:T(8,128)(2,1)} %reshape.230) | copy-start | bytes 1966084
  87.3 5.2 %copy-start.8 = (bf16[1,64,2048]{2,1,0:T(8,128)(2,1)S(1)}, bf16[1,64,2048]{2,1,0:T(8,128)(2,1)}, u32[]{:S(2)}) copy-start(bf16[1,64,2048]{2,1,0:T(8,128)(2,1)} %param.11) | copy-start | bytes 786436
  88.3 25.2 %all-to-all-start.4 = ((bf16[8,20,2048]{2,1,0:T(8,128)(2,1)}), bf16[8,20,2048]{2,1,0:T(8,128)(2,1)S(1)}, u32[]{:S(2)}, u32[]{:S(2)}) async-start(bf16[8,20,2048]{2,1,0:T(8,128)(2,1)} %reshape.231), calls=%async_computation.4 | async-start | bytes 1572864 | tf_op jit(solution)/shard_map/all_to_all | solution.py:132
  92.5 21.1 %copy-start.22 = (s32[128]{0:T(128)}, s32[128]{0:T(128)S(1)}, u32[]{:S(2)}) copy-start(s32[128]{0:T(128)S(1)} %select_reduce_fusion.1) | copy-start | bytes 1540
  114.6 2.0 copy-start.5
  116.6 2.5 %copy-start.3 = (f32[64,2048]{1,0:T(8,128)}, f32[64,2048]{1,0:T(8,128)S(1)}, u32[]{:S(2)}) copy-start(f32[64,2048]{1,0:T(8,128)S(1)} %reduce_sum.83) | copy-start | bytes 1572868
  121.1 29.9 %copy-start.2 = (bf16[1,1,2048,384]{3,2,1,0:T(8,128)(2,1)S(1)}, bf16[1,1,2048,384]{3,2,1,0:T(8,128)(2,1)}, u32[]{:S(2)}) copy-start(bf16[1,1,2048,384]{3,2,1,0:T(8,128)(2,1)} %param.19) | copy-start | bytes 4718596
  156.0 4.9 %copy-start.19 = (f32[1,64,2]{1,2,0:T(2,128)S(1)}, f32[1,64,2]{1,2,0:T(2,128)}, u32[]{:S(2)}) copy-start(f32[1,64,2]{1,2,0:T(2,128)} %param.16) | copy-start | bytes 1540
  156.0 5.6 %copy-start.23 = (s32[128]{0:T(128)S(1)}, s32[128]{0:T(128)}, u32[]{:S(2)}) copy-start(s32[128]{0:T(128)} %copy-done.22) | copy-start | bytes 1540
  156.0 5.6 %copy-start.21 = (f32[64]{0:T(128)S(1)}, f32[64]{0:T(128)}, u32[]{:S(2)}) copy-start(f32[64]{0:T(128)} %copy-done.20) | copy-start | bytes 772
  156.0 5.6 %copy-start.24 = (f32[64]{0:T(128)S(1)}, f32[64]{0:T(128)}, u32[]{:S(2)}) copy-start(f32[64]{0:T(128)} %get-tuple-element.8) | copy-start | bytes 772
  156.0 5.6 %copy-start.4 = (f32[64,2048]{1,0:T(8,128)S(1)}, f32[64,2048]{1,0:T(8,128)}, u32[]{:S(2)}) copy-start(f32[64,2048]{1,0:T(8,128)} %copy-done.3) | copy-start | bytes 1572868
  156.1 5.6 %copy-start.11 = (bf16[1,64,2048]{2,1,0:T(8,128)(2,1)S(1)}, bf16[1,64,2048]{2,1,0:T(8,128)(2,1)}, u32[]{:S(2)}) copy-start(bf16[1,64,2048]{2,1,0:T(8,128)(2,1)} %param.13) | copy-start | bytes 786436
  157.1 26.5 %all-to-all-start.1 = ((bf16[8,20,2048]{2,1,0:T(8,128)(2,1)}), bf16[8,20,2048]{2,1,0:T(8,128)(2,1)S(1)}, u32[]{:S(2)}, u32[]{:S(2)}) async-start(bf16[8,20,2048]{2,1,0:T(8,128)(2,1)} %reshape.224), calls=%async_computation.1 | async-start | bytes 1572864 | tf_op jit(solution)/shard_map/all_to_all | solution.py:125
  162.6 26.3 %collective-permute-start.1 = (bf16[1,64,2048]{2,1,0:T(8,128)(2,1)}, bf16[1,64,2048]{2,1,0:T(8,128)(2,1)S(1)}, u32[]{:S(2)}, u32[]{:S(2)}) collective-permute-start(bf16[1,64,2048]{2,1,0:T(8,128)(2,1)} %fusion.49), channel_id=1, source_target_pairs={{8,0},{16,8},{24,16},{32,24},{40,32},{48,40},{56,48},{0,56},{9,1},... | collective-permute-start | bytes 786440 | tf_op jit(solution)/shard_map/ppermute | solution.py:18
  185.5 3.3 %copy-start.9 = (bf16[1,64,2048]{2,1,0:T(8,128)(2,1)S(1)}, bf16[1,64,2048]{2,1,0:T(8,128)(2,1)}, u32[]{:S(2)}) copy-start(bf16[1,64,2048]{2,1,0:T(8,128)(2,1)} %param.11) | copy-start | bytes 786436
  188.9 7.0 %collective-permute-start = (bf16[1,64,2048]{2,1,0:T(8,128)(2,1)S(1)}, bf16[1,64,2048]{2,1,0:T(8,128)(2,1)S(1)}, u32[]{:S(2)}, u32[]{:S(2)}) collective-permute-start(bf16[1,64,2048]{2,1,0:T(8,128)(2,1)S(1)} %fusion.48), channel_id=1, source_target_pairs={{0,8},{8,16},{16,24},{24,32},{32,40},{40,48},{48,56},{56,0},{1,9},... | collective-permute-start | bytes 786440 | tf_op jit(solution)/shard_map/ppermute | solution.py:15
  (8 other events, 10.1 us)
Sparse Core Ops, SparseCore 0:
  84.9 80.6 reduce-scatter.1
where the time goes:
time: 207 us; the launch traced here: 206 us
  waiting for transfers between devices  88.6 us (43%)
  blocking collectives  27.9 us (13%)
  local copies, waits for them, and re-layouts  26.6 us (13%)
  starting transfers between devices  20.5 us (10%)
  matrix products  16.3 us (8%)
  between operations  14.6 us (7%)
  other arithmetic  11.5 us (6%)
    all_to_all x1, blocking collectives, shards(): lax.all_to_all(send_fwd.reshape(experts, capacity, width), 'expert', spli...  27.9 us
    all_to_all x1, waiting for transfers between devices, shards(): lax.all_to_all(send_bwd, 'expert', split_axis=0, concat_axis=0, tiled=True)  22.2 us
    all_to_all x1, waiting for transfers between devices, shards(): lax.all_to_all(slot_grad.reshape(experts, capacity, width), 'expert', spl...  20.3 us
    all_to_all x1, waiting for transfers between devices, shards(): lax.all_to_all(send_grad, 'expert', split_axis=0, concat_axis=0, tiled=True)  19.9 us
    all_to_all x1, waiting for transfers between devices, shards(): lax.all_to_all(out_fwd.reshape(experts, capacity, width), 'expert', split...  19.2 us
    all_to_all x1, starting transfers between devices, shards(): lax.all_to_all(send_bwd, 'expert', split_axis=0, concat_axis=0, tiled=True)  7.1 us
    ppermute x1, waiting for transfers between devices, padded(): lax.ppermute(lax.slice_in_dim(block, block.shape[dim] - width, None, axis...  6.98 us
    all_to_all x1, starting transfers between devices, shards(): lax.all_to_all(send_grad, 'expert', split_axis=0, concat_axis=0, tiled=True)  4.21 us
  transfers between devices with their start and end apart: 7, of which 5 were waited for; matrix products, arithmetic and copies ran while one was open for 15% of the time, Pallas kernels for 0%

commit v1 on v0

v1 whole, which is shorter than its diff:
```python
import functools

import jax
import jax.numpy as jnp
from jax import lax
from jax.experimental import pallas as pl
from jax.experimental.pallas import tpu as pltpu
from jax.sharding import PartitionSpec as P

EPS = 1e-06
NOWHERE = -1000.0
CHUNK = 512
CONTRACT_FIRST = (((0,), (0,)), ((), ()))
CONTRACT_LAST = (((1,), (1,)), ((), ()))
HBM = pl.BlockSpec(memory_space=pltpu.HBM)


def matmul(a, b, dims=(((1,), (0,)), ((), ()))):
    return lax.dot_general(a, b, dims, preferred_element_type=jnp.float32)


def slot_table(ids, experts):
    tokens = ids.shape[1]
    expert = lax.broadcasted_iota(jnp.int32, (experts, tokens), 0)
    picks = [ids[k : k + 1, :] == expert for k in range(ids.shape[0])]
    member = functools.reduce(jnp.logical_or, picks)
    source = lax.broadcasted_iota(jnp.int32, (tokens, tokens), 0)
    target = lax.broadcasted_iota(jnp.int32, (tokens, tokens), 1)
    earlier = jnp.where(source < target, 1.0, 0.0).astype(jnp.bfloat16)
    before = matmul(jnp.where(member, 1.0, 0.0).astype(jnp.bfloat16), earlier)
    return picks, member, before


def spread(table, block):
    return jnp.concatenate(
        [jnp.broadcast_to(table[e : e + 1, :], (block, table.shape[1])) for e in range(table.shape[0])],
        axis=0,
    )


def slot_of_row(experts, block, tokens):
    one = lax.broadcasted_iota(jnp.int32, (block, tokens), 0).astype(jnp.float32)
    return jnp.concatenate([one] * experts, axis=0)


def onehot(mask):
    return jnp.where(mask, 1.0, 0.0).astype(jnp.bfloat16)


def start_all(pairs, sems):
    copies = [
        pltpu.make_async_copy(source, target, sems.at[i]) for i, (source, target) in enumerate(pairs)
    ]
    for copy in copies:
        copy.start()
    return copies


def wait_all(copies):
    for copy in copies:
        copy.wait()


def store_columns(stores, source, target, at, width, sems):
    cols = pl.ds(at, width)
    copy = pltpu.make_async_copy(source.at[:, cols], target.at[:, cols], sems.at[len(stores)])
    copy.start()
    stores.append(copy)


def row_factor(ref):
    width = ref.shape[1]
    total = jnp.zeros((ref.shape[0], 1), jnp.float32)
    for at in range(0, width, CHUNK):
        part = ref[:, at : at + CHUNK].astype(jnp.float32)
        total = total + jnp.sum(part * part, axis=1, keepdims=True)
    return lax.rsqrt(total / width + EPS)


def pack_bwd(experts, cap, ids_hbm, gates_hbm, saved_hbm, grad_hbm, gain_hbm, out_hbm, ids_ref, gates_ref, saved_ref, grad_ref, gain_ref, out_ref, sems, out_sems):
    copies = start_all(
        [
            (ids_hbm, ids_ref),
            (gates_hbm, gates_ref),
            (saved_hbm, saved_ref),
            (gain_hbm, gain_ref),
            (grad_hbm, grad_ref),
        ],
        sems,
    )
    wait_all(copies[:2])
    ids = ids_ref[...]
    tokens = ids.shape[1]
    block = 2 * cap
    picks, member, before = slot_table(ids, experts)
    rows = spread(jnp.where(member, before, NOWHERE), block)
    slot = slot_of_row(experts, block, tokens)
    hit_x = rows == slot
    hit_g = rows + cap == slot
    gate = spread(jnp.where(picks[0], gates_ref[0:1, :], gates_ref[1:2, :]), block)
    scale = jnp.sum(
        jnp.where(hit_x, 1.0, 0.0) + jnp.where(hit_g, gate, 0.0), axis=1, keepdims=True
    )
    place_x, place_g = onehot(hit_x), onehot(hit_g)
    wait_all(copies[2:])
    factor = row_factor(saved_ref)
    stores = []
    for at in range(0, saved_ref.shape[1], CHUNK):
        cols = slice(at, at + CHUNK)
        normed = (saved_ref[:, cols].astype(jnp.float32) * factor * gain_ref[:, cols]).astype(
            jnp.bfloat16
        )
        placed = matmul(place_x, normed) + matmul(place_g, grad_ref[:, cols])
        out_ref[:, cols] = (placed * scale).astype(jnp.bfloat16)
        store_columns(stores, out_ref, out_hbm, at, CHUNK, out_sems)
    wait_all(stores)


def pack_fwd(experts, cap, ids_hbm, act_hbm, gain_hbm, out_hbm, ids_ref, act_ref, gain_ref, out_ref, sems, out_sems):
    copies = start_all([(ids_hbm, ids_ref), (act_hbm, act_ref), (gain_hbm, gain_ref)], sems)
    wait_all(copies)
    ids = ids_ref[...]
    tokens = ids.shape[1]
    block = 2 * cap
    half = act_ref.shape[1] // 2
    _, member, before = slot_table(ids, experts)
    rows = spread(jnp.where(member, before, NOWHERE), block)
    slot = slot_of_row(experts, block, tokens)
    place_low, place_high = onehot(rows == slot), onehot(rows + cap == slot)
    factor = row_factor(act_ref)
    stores = []
    for at in range(0, half, CHUNK):
        low, high = slice(at, at + CHUNK), slice(half + at, half + at + CHUNK)
        normed_low = (act_ref[:, low].astype(jnp.float32) * factor * gain_ref[:, low]).astype(
            jnp.bfloat16
        )
        normed_high = (act_ref[:, high].astype(jnp.float32) * factor * gain_ref[:, high]).astype(
            jnp.bfloat16
        )
        out_ref[:, low] = (
            matmul(place_low, normed_low) + matmul(place_high, normed_high)
        ).astype(jnp.bfloat16)
        store_columns(stores, out_ref, out_hbm, at, CHUNK, out_sems)
    wait_all(stores)


def first_rows(shape, cap):
    row = lax.broadcasted_iota(jnp.int32, shape, 0)
    return lax.rem(row, 2 * cap) < cap


def expert_bwd(cap, scale, recv_hbm, gate_hbm, up_hbm, down_hbm, right_hbm, partial_hbm, recv_ref, right_ref, gate_ref, up_ref, down_ref, pre_g, pre_u, grad, out_ref, sems, out_sems):
    hid = gate_ref.shape[1]
    slots = recv_ref.shape[0]
    copies = start_all(
        [
            (recv_hbm, recv_ref),
            (down_hbm, down_ref),
            (gate_hbm, gate_ref),
            (up_hbm, up_ref),
        ],
        sems,
    )
    wait_all(copies[:2])
    grad[...] = matmul(recv_ref[...], down_ref[...], CONTRACT_LAST)
    copies[2].wait()
    pre_g[...] = matmul(recv_ref[...], gate_ref[...])
    copies[3].wait()
    pre_u[...] = matmul(recv_ref[...], up_ref[...])
    for at in range(0, hid, 128):
        cols = slice(at, at + 128)
        gate, up = pre_g[:, cols], pre_u[:, cols]
        hidden_grad = pltpu.roll(grad[:, cols], slots - cap, 0)
        first = first_rows(gate.shape, cap)
        sig = 1.0 / (1.0 + jnp.exp(-gate))
        silu = gate * sig
        zero = jnp.zeros_like(gate)
        gate_grad = hidden_grad * up * sig * (1.0 + gate * (1.0 - sig))
        right_ref[:, at : at + 128] = jnp.where(first, gate_grad, zero).astype(jnp.bfloat16)
        right_ref[:, hid + at : hid + at + 128] = jnp.where(
            first, hidden_grad * silu, zero
        ).astype(jnp.bfloat16)
        hidden = pltpu.roll(jnp.where(first, silu * up, zero), cap, 0)
        right_ref[:, 2 * hid + at : 2 * hid + at + 128] = hidden.astype(jnp.bfloat16)
    kept = pltpu.make_async_copy(right_ref, right_hbm, out_sems.at[2])
    kept.start()
    rows = out_ref.shape[1]
    stores = []
    for i in range(partial_hbm.shape[0] // rows):
        slot = i % 2
        if i >= 2:
            stores[i - 2].wait()
        left = recv_ref[:, i * rows : (i + 1) * rows]
        out_ref[slot] = (matmul(left, right_ref[...], CONTRACT_FIRST) * scale).astype(jnp.bfloat16)
        store = pltpu.make_async_copy(
            out_ref.at[slot], partial_hbm.at[pl.ds(i * rows, rows), :], out_sems.at[slot]
        )
        store.start()
        stores.append(store)
    wait_all(stores[-2:] + [kept])


def expert_fwd(cap, recv_hbm, right_hbm, gate_hbm, up_hbm, down_hbm, out_hbm, recv_ref, right_ref, out_ref, gate_ref, up_ref, down_ref, low_g, low_u, high_g, high_u, hid_ref, sems, out_sems):
    hid = gate_ref.shape[1]
    slots, half = recv_ref.shape
    copies = start_all(
        [
            (recv_hbm, recv_ref),
            (gate_hbm, gate_ref),
            (up_hbm, up_ref),
            (right_hbm, right_ref),
            (down_hbm, down_ref),
        ],
        sems,
    )
    wait_all(copies[:2])
    low_g[...] = matmul(recv_ref[...], gate_ref[:half, :])
    high_g[...] = matmul(recv_ref[...], gate_ref[half:, :])
    copies[2].wait()
    low_u[...] = matmul(recv_ref[...], up_ref[:half, :])
    high_u[...] = matmul(recv_ref[...], up_ref[half:, :])
    for at in range(0, hid, 128):
        cols = slice(at, at + 128)
        gate = low_g[:, cols] + pltpu.roll(high_g[:, cols], slots - cap, 0)
        up = low_u[:, cols] + pltpu.roll(high_u[:, cols], slots - cap, 0)
        hidden = gate / (1.0 + jnp.exp(-gate)) * up
        hidden = jnp.where(first_rows(gate.shape, cap), hidden, jnp.zeros_like(hidden))
        hid_ref[:, cols] = pltpu.roll(hidden, cap, 0).astype(jnp.bfloat16)
    wait_all(copies[3:])
    stores = []
    for at in range(0, out_ref.shape[1], CHUNK):
        cols = slice(at, at + CHUNK)
        total = matmul(hid_ref[...], down_ref[:, cols])
        total = total + matmul(right_ref[:, :hid], gate_ref[cols, :], CONTRACT_LAST)
        total = total + matmul(right_ref[:, hid : 2 * hid], up_ref[cols, :], CONTRACT_LAST)
        out_ref[:, cols] = total.astype(jnp.bfloat16)
        store_columns(stores, out_ref, out_hbm, at, CHUNK, out_sems)
    wait_all(stores)


def as_column(row):
    count = row.shape[1]
    down = lax.broadcasted_iota(jnp.int32, (count, count), 0)
    across = lax.broadcasted_iota(jnp.int32, (count, count), 1)
    kept = jnp.where(down == across, jnp.broadcast_to(row, (count, count)), 0.0)
    return jnp.sum(kept, axis=1, keepdims=True)


def combine(experts, cap, back_hbm, fwd_ids_hbm, bwd_ids_hbm, gates_hbm, act_hbm, saved_hbm, grad_hbm, gain_hbm, act_out_hbm, grad_out_hbm, act_out_ref, grad_out_ref, back_ref, fwd_ids_ref, bwd_ids_ref, gates_ref, act_ref, saved_ref, grad_ref, gain_ref, wide, sems, out_sems):
    copies = start_all(
        [
            (fwd_ids_hbm, fwd_ids_ref),
            (bwd_ids_hbm, bwd_ids_ref),
            (gates_hbm, gates_ref),
            (back_hbm, back_ref),
            (saved_hbm, saved_ref),
            (gain_hbm, gain_ref),
            (act_hbm, act_ref),
            (grad_hbm, grad_ref),
        ],
        sems,
    )
    wait_all(copies[:3])
    tokens, width = act_ref.shape
    block = 2 * cap
    slot = slot_of_row(experts, block, tokens)
    picks, _, before = slot_table(fwd_ids_ref[...], experts)
    chosen = [onehot(spread(jnp.where(pick, before, NOWHERE), block) + cap == slot) for pick in picks]
    gates = [as_column(gates_ref[k : k + 1, :]) for k in range(len(picks))]
    _, member, before = slot_table(bwd_ids_ref[...], experts)
    both = onehot(spread(jnp.where(member, before, NOWHERE), block) == slot)
    wait_all(copies[3:])
    factor = row_factor(saved_ref)
    inner = jnp.zeros((tokens, 1), jnp.float32)
    for at in range(0, width, CHUNK):
        cols = slice(at, at + CHUNK)
        back = back_ref[:, cols]
        total = gates[0] * matmul(chosen[0], back, CONTRACT_FIRST)
        total = total + gates[1] * matmul(chosen[1], back, CONTRACT_FIRST)
        act_out_ref[:, cols] = (act_ref[:, cols].astype(jnp.float32) + total).astype(jnp.bfloat16)
        scaled = matmul(both, back, CONTRACT_FIRST) * gain_ref[:, cols]
        wide[:, cols] = scaled
        inner = inner + jnp.sum(
            saved_ref[:, cols].astype(jnp.float32) * scaled, axis=1, keepdims=True
        )
    stores = []
    store_columns(stores, act_out_ref, act_out_hbm, 0, width, out_sems)
    pull = inner / width * factor * factor * factor
    for at in range(0, width, CHUNK):
        cols = slice(at, at + CHUNK)
        value = grad_ref[:, cols].astype(jnp.float32) + (
            wide[:, cols] * factor - saved_ref[:, cols].astype(jnp.float32) * pull
        )
        grad_out_ref[:, cols] = value.astype(jnp.bfloat16)
        store_columns(stores, grad_out_ref, grad_out_hbm, at, CHUNK, out_sems)
    wait_all(stores)


PARAMS = pltpu.CompilerParams(vmem_limit_bytes=66_800_000)


def cost(flops, moved):
    return pl.CostEstimate(flops=flops, bytes_accessed=moved, transcendentals=0)


def exchange(rows, experts):
    blocks = rows.reshape(experts, -1, rows.shape[-1])
    moved = lax.all_to_all(blocks, "expert", split_axis=0, concat_axis=0, tiled=True)
    return moved.reshape(rows.shape)


def shards(
    act_in,
    saved_in,
    grad_in,
    fwd_ids,
    bwd_ids,
    fwd_gates,
    bwd_gates,
    norm_gain,
    w_gate,
    w_up,
    w_down,
):
    experts = lax.axis_size("expert")
    replicas = lax.axis_size("dp")
    sections = lax.axis_size("section")
    tokens, width = act_in.shape[1:]
    topk = fwd_ids.shape[2]
    cap = min(tokens, 5 * tokens * topk // (4 * experts))
    slots = 2 * cap * experts
    here, saved, upstream = act_in[0], saved_in[0], grad_in[0]
    weight_gate, weight_up, weight_down = w_gate[0, 0], w_up[0, 0], w_down[0, 0]
    hid = weight_gate.shape[1]
    ids_fwd, ids_bwd = fwd_ids[0].T, bwd_ids[0].T
    gates_fwd, gates_bwd = fwd_gates[0].T, bwd_gates[0].T
    small = tokens * width * 2
    big = slots * width * 2
    weight_bytes = 3 * width * hid * 2
    ids_buf = pltpu.VMEM((topk, tokens), jnp.int32)
    gates_buf = pltpu.VMEM((topk, tokens), jnp.float32)
    rows_buf = pltpu.VMEM((tokens, width), jnp.bfloat16)
    gain_buf = pltpu.VMEM((1, width), jnp.float32)
    slots_buf = pltpu.VMEM((slots, width), jnp.bfloat16)
    half_buf = pltpu.VMEM((slots, width // 2), jnp.bfloat16)
    right_buf = pltpu.VMEM((slots, 3 * hid), jnp.bfloat16)
    chunks = width // CHUNK
    dma = lambda count: pltpu.SemaphoreType.DMA((count,))
    weight_bufs = [
        pltpu.VMEM((width, hid), jnp.bfloat16),
        pltpu.VMEM((width, hid), jnp.bfloat16),
        pltpu.VMEM((hid, width), jnp.bfloat16),
    ]

    send_bwd = pl.pallas_call(
        functools.partial(pack_bwd, experts, cap),
        out_shape=jax.ShapeDtypeStruct((slots, width), jnp.bfloat16),
        in_specs=[HBM] * 5,
        out_specs=HBM,
        scratch_shapes=[ids_buf, gates_buf, rows_buf, rows_buf, gain_buf, slots_buf, dma(5), dma(chunks)],
        compiler_params=PARAMS,
        cost_estimate=cost(4 * slots * tokens * width, 2 * small + big),
        name="pack_bwd",
    )(ids_bwd, gates_bwd, saved, upstream, norm_gain)
    recv_bwd = exchange(send_bwd, experts)
    send_fwd = pl.pallas_call(
        functools.partial(pack_fwd, experts, cap),
        out_shape=jax.ShapeDtypeStruct((slots, width // 2), jnp.bfloat16),
        in_specs=[HBM] * 3,
        out_specs=HBM,
        scratch_shapes=[ids_buf, rows_buf, gain_buf, half_buf, dma(3), dma(chunks)],
        compiler_params=PARAMS,
        cost_estimate=cost(2 * slots * tokens * width, small + big // 2),
        name="pack_fwd",
    )(ids_fwd, here, norm_gain)
    send_fwd, recv_bwd = lax.optimization_barrier((send_fwd, recv_bwd))
    recv_fwd = exchange(send_fwd, experts)

    right, partial = pl.pallas_call(
        functools.partial(expert_bwd, cap, 1.0 / replicas),
        out_shape=(
            jax.ShapeDtypeStruct((slots, 3 * hid), jnp.bfloat16),
            jax.ShapeDtypeStruct((width, 3 * hid), jnp.bfloat16),
        ),
        in_specs=[HBM] * 4,
        out_specs=(HBM, HBM),
        scratch_shapes=[slots_buf, right_buf]
        + weight_bufs
        + [pltpu.VMEM((slots, hid), jnp.float32)] * 3
        + [
            pltpu.VMEM((2, 256, 3 * hid), jnp.bfloat16),
            dma(4),
            dma(3),
        ],
        compiler_params=PARAMS,
        cost_estimate=cost(12 * slots * width * hid, big + 2 * weight_bytes),
        name="expert_bwd",
    )(recv_bwd, weight_gate, weight_up, weight_down)
    summed = lax.psum_scatter(partial, "dp", scatter_dimension=0, tiled=True)

    back = pl.pallas_call(
        functools.partial(expert_fwd, cap),
        out_shape=jax.ShapeDtypeStruct((slots, width), jnp.bfloat16),
        in_specs=[HBM] * 5,
        out_specs=HBM,
        scratch_shapes=[half_buf, right_buf, slots_buf]
        + weight_bufs
        + [pltpu.VMEM((slots, hid), jnp.float32)] * 4
        + [pltpu.VMEM((slots, hid), jnp.bfloat16), dma(5), dma(chunks)],
        compiler_params=PARAMS,
        cost_estimate=cost(10 * slots * width * hid, 2 * big + weight_bytes),
        name="expert_fwd",
    )(recv_fwd, right, weight_gate, weight_up, weight_down)
    returned = exchange(back, experts)

    layer_out, input_grad = pl.pallas_call(
        functools.partial(combine, experts, cap),
        out_shape=(
            jax.ShapeDtypeStruct((tokens, width), jnp.bfloat16),
            jax.ShapeDtypeStruct((tokens, width), jnp.bfloat16),
        ),
        in_specs=[HBM] * 8,
        out_specs=(HBM, HBM),
        scratch_shapes=[rows_buf, rows_buf, slots_buf, ids_buf, ids_buf, gates_buf, rows_buf, rows_buf, rows_buf, gain_buf]
        + [pltpu.VMEM((tokens, width), jnp.float32), dma(8), dma(chunks + 1)],
        compiler_params=PARAMS,
        cost_estimate=cost(6 * slots * tokens * width, big + 5 * small),
        name="combine",
    )(returned, ids_fwd, ids_bwd, gates_fwd, here, saved, upstream, norm_gain)
    ring = [(i, (i + 1) % sections) for i in range(sections)]
    act_out = lax.ppermute(layer_out, "section", ring)
    grad_out = lax.ppermute(input_grad, "section", [(target, source) for source, target in ring])
    return (act_out[None], grad_out[None], summed.astype(jnp.float32)[None, None])


def solution(mesh):
    tokens = P("section", ("dp", "expert"), None)
    weights = P("section", "expert", None, None)
    in_specs = (tokens,) * 7 + (P("section", None),) + (weights,) * 3
    out_specs = (tokens, tokens, P("section", "expert", "dp", None))

    return jax.shard_map(shards, mesh=mesh, in_specs=in_specs, out_specs=out_specs, check_vma=False)
```

time: 207 us -> 162 us (0.78)
  the two profiles are of different devices: /device:TPU:448 before, /device:TPU:2 now
where the time goes in v1:
time: 162 us; the launch traced here: 161 us
  blocking collectives  62.1 us (38%)
  waiting for transfers between devices  46.2 us (29%)
  Pallas kernels  25.8 us (16%)
  between operations  14.1 us (9%)
  starting transfers between devices  8.9 us (5%)
  local copies, waits for them, and re-layouts  2.46 us (2%)
  other arithmetic  1.81 us (1%)
    all_to_all x2, blocking collectives, exchange(): lax.all_to_all(blocks, 'expert', split_axis=0, concat_axis=0, tiled=True)  62.1 us
    all_to_all x1, waiting for transfers between devices, exchange(): lax.all_to_all(blocks, 'expert', split_axis=0, concat_axis=0, tiled=True)  32.1 us
    pallas_call x1, Pallas kernels, shards(): pl.pallas_call(functools.partial(expert_bwd, cap, 1.0 / replicas), out_sh...  10.6 us
    reduce_scatter x1, waiting for transfers between devices, shards(): summed = lax.psum_scatter(partial, 'dp', scatter_dimension=0, tiled=True)  9.85 us
    all_to_all x1, starting transfers between devices, exchange(): lax.all_to_all(blocks, 'expert', split_axis=0, concat_axis=0, tiled=True)  7.11 us
    pallas_call x1, Pallas kernels, shards(): pl.pallas_call(functools.partial(expert_fwd, cap), out_shape=jax.ShapeDty...  6.55 us
    ppermute x1, waiting for transfers between devices, shards(): act_out = lax.ppermute(layer_out, 'section', ring)  4.26 us
    pallas_call x1, Pallas kernels, shards(): pl.pallas_call(functools.partial(combine, experts, cap), out_shape=(jax.S...  3.45 us
  transfers between devices with their start and end apart: 4, of which 3 were waited for; matrix products, arithmetic and copies ran while one was open for 0% of the time, Pallas kernels for 8%

profile of v1, /device:TPU:2, one launch (start us, length us, event | category | flops | bytes accessed | tf_op | source)
XLA Modules:
  0.0 161.3 jit_solution(9230896687631313580)
XLA Ops:
  7.2 2.8 %pack_bwd.1 = bf16[320,2048]{1,0:T(8,128)(2,1)} custom-call(s32[2,64]{1,0:T(2,128)} %bitcast.42, f32[2,64]{1,0:T(2,128)} %bitcast.46, bf16[64,2048]{1,0:T(8,128)(2,1)} %bitcast.35, bf16[64,2048]{1,0:T(8,128)(2,1)} %bitcast.37, f32[1,2048]{1,0:T(1,128)} %gain_hbm.5), custom_call_target="tpu_custom_call" | custom-call | flops 167772160 | bytes 1835008 | tf_op jit(solution)/shard_map/pack_bwd/pallas_call | solution.py:355
  9.9 7.1 %all-to-all-start = ((bf16[8,40,2048]{2,1,0:T(8,128)(2,1)}), bf16[8,40,2048]{2,1,0:T(8,128)(2,1)}, u32[]{:S(2)}, u32[]{:S(2)}) async-start(bf16[8,40,2048]{2,1,0:T(8,128)(2,1)} %bitcast.29), calls=%async_computation | async-start | bytes 2621440 | tf_op jit(solution)/shard_map/all_to_all | solution.py:308
  17.1 0.0 reduce-scatter.2.cloned.1.call-start
  17.1 2.4 %pack_fwd.1 = bf16[320,1024]{1,0:T(8,128)(2,1)} custom-call(s32[2,64]{1,0:T(2,128)} %bitcast.44, bf16[64,2048]{1,0:T(8,128)(2,1)} %bitcast.33, f32[1,2048]{1,0:T(1,128)} %gain_hbm.5), custom_call_target="tpu_custom_call" | custom-call | flops 83886080 | bytes 917504 | tf_op jit(solution)/shard_map/pack_fwd/pallas_call | solution.py:366
  19.5 32.1 %all-to-all-done = bf16[8,40,2048]{2,1,0:T(8,128)(2,1)} async-done(((bf16[8,40,2048]{2,1,0:T(8,128)(2,1)}), bf16[8,40,2048]{2,1,0:T(8,128)(2,1)}, u32[]{:S(2)}, u32[]{:S(2)}) %all-to-all-start) | async-done | bytes 1310752 | tf_op jit(solution)/shard_map/all_to_all | solution.py:308
  51.6 10.6 %expert_bwd.1 = (bf16[320,1152]{1,0:T(8,128)(2,1)}, bf16[2048,1152]{1,0:T(8,128)(2,1)}) custom-call(bf16[320,2048]{1,0:T(8,128)(2,1)} %bitcast.10.recv_hbm, bf16[2048,384]{1,0:T(8,128)(2,1)} %bitcast.48, bf16[2048,384]{1,0:T(8,128)(2,1)} %bitcast.50, bf16[384,2048]{1,0:T(8,128)(2,1)} %bitcast.52), custom_call_target="tpu_custom_call" | custom-call | flops 3019898880 | bytes 10747904 | tf_op jit(solution)/shard_map/expert_bwd/pallas_call | solution.py:379
  62.2 0.0 copy-start
  62.3 0.0 reduce-scatter.2.cloned.1.call-update
  62.3 1.1 copy-done
  63.3 23.8 %all_to_all.15 = bf16[8,40,1024]{2,1,0:T(8,128)(2,1)} all-to-all(bf16[8,40,1024]{2,1,0:T(8,128)(2,1)S(1)} %bitcast.31), channel_id=1, replica_groups=mesh['dp'=16,'section'=8,'expert'=8] {'expert'}, dimensions={0} | all-to-all | bytes 1310720 | tf_op jit(solution)/shard_map/all_to_all | solution.py:308
  87.2 6.5 %expert_fwd.1 = bf16[320,2048]{1,0:T(8,128)(2,1)} custom-call(bf16[320,1024]{1,0:T(8,128)(2,1)} %bitcast.39, bf16[320,1152]{1,0:T(8,128)(2,1)} %get-tuple-element.11.right_hbm, bf16[2048,384]{1,0:T(8,128)(2,1)} %bitcast.49, bf16[2048,384]{1,0:T(8,128)(2,1)} %bitcast.51, bf16[384,2048]{1,0:T(8,128)(2,1)} %bitcast.53), custom_call_target="tpu_custom_call" | custom-call | flops 2516582400 | bytes 7340032 | tf_op jit(solution)/shard_map/expert_fwd/pallas_call | solution.py:401
  93.7 38.2 %all_to_all.16 = bf16[8,40,2048]{2,1,0:T(8,128)(2,1)} all-to-all(bf16[8,40,2048]{2,1,0:T(8,128)(2,1)} %bitcast.32), channel_id=1, replica_groups=mesh['dp'=16,'section'=8,'expert'=8] {'expert'}, dimensions={0} | all-to-all | bytes 2621440 | tf_op jit(solution)/shard_map/all_to_all | solution.py:308
  132.0 3.4 %combine.1 = (bf16[64,2048]{1,0:T(8,128)(2,1)}, bf16[64,2048]{1,0:T(8,128)(2,1)}) custom-call(bf16[320,2048]{1,0:T(8,128)(2,1)} %bitcast.30, s32[2,64]{1,0:T(2,128)} %bitcast.45, s32[2,64]{1,0:T(2,128)} %bitcast.43, f32[2,64]{1,0:T(2,128)} %bitcast.47, bf16[64,2048]{1,0:T(8,128)(2,1)} %bitcast.34, bf16[64,2048]{1,0:T(8,128)(2,1)} %bitcast.36, ...), custom_call_target="tpu_custom_call" | custom-call | flops 251658240 | bytes 2621440 | tf_op jit(solution)/shard_map/combine/pallas_call | solution.py:416
  135.4 0.0 collective-permute-start
  135.4 1.7 %collective-permute-start.1 = (bf16[64,2048]{1,0:T(8,128)(2,1)}, bf16[64,2048]{1,0:T(8,128)(2,1)S(1)}, u32[]{:S(2)}, u32[]{:S(2)}) collective-permute-start(bf16[64,2048]{1,0:T(8,128)(2,1)} %get-tuple-element.13), channel_id=1, source_target_pairs={{8,0},{16,8},{24,16},{32,24},{40,32},{48,40},{56,48},{0,56},{9,1},... | collective-permute-start | bytes 786440 | tf_op jit(solution)/shard_map/ppermute | solution.py:432
  137.2 4.3 %collective-permute-done = bf16[64,2048]{1,0:T(8,128)(2,1)S(1)} collective-permute-done((bf16[64,2048]{1,0:T(8,128)(2,1)}, bf16[64,2048]{1,0:T(8,128)(2,1)S(1)}, u32[]{:S(2)}, u32[]{:S(2)}) %collective-permute-start) | collective-permute-done | bytes 262176 | tf_op jit(solution)/shard_map/ppermute | solution.py:431
  141.4 0.0 collective-permute-done.1
  141.4 9.9 %reduce-scatter.2.cloned.1.call-done = bf16[128,1152]{1,0:T(8,128)(2,1)} async-done(((bf16[2048,1152]{1,0:T(8,128)(2,1)}), bf16[128,1152]{1,0:T(8,128)(2,1)}) %reduce-scatter.2.cloned.1.call-update) | async-done | bytes 294928 | tf_op jit(solution)/shard_map/reduce_scatter | solution.py:399
  151.3 1.8 %bitcast_convert_fusion = f32[1,1,128,1152]{3,2,1,0:T(8,128)} fusion(bf16[128,1152]{1,0:T(8,128)(2,1)} %reduce-scatter.2.cloned.1.call-done), kind=kLoop, calls=%fused_computation | loop fusion | flops 147456 | bytes 884736 | tf_op jit(solution)/shard_map/broadcast_in_dim | solution.py:433
  153.1 0.7 copy.16
  153.8 0.7 copy.17
Async XLA Ops:
  9.9 41.7 %all-to-all-start = ((bf16[8,40,2048]{2,1,0:T(8,128)(2,1)}), bf16[8,40,2048]{2,1,0:T(8,128)(2,1)}, u32[]{:S(2)}, u32[]{:S(2)}) async-start(bf16[8,40,2048]{2,1,0:T(8,128)(2,1)} %bitcast.29), calls=%async_computation | async-start | bytes 2621440 | tf_op jit(solution)/shard_map/all_to_all | solution.py:308
  17.1 134.2 %reduce-scatter.2.cloned.1.call-start = ((), (), s32[]{:S(2)}) async-start(), calls=%async_computation.4 | async-start | bytes 5013504 | tf_op jit(solution)/shard_map/reduce_scatter | solution.py:399
  62.2 1.1 copy-start
  135.4 6.0 %collective-permute-start = (bf16[64,2048]{1,0:T(8,128)(2,1)}, bf16[64,2048]{1,0:T(8,128)(2,1)S(1)}, u32[]{:S(2)}, u32[]{:S(2)}) collective-permute-start(bf16[64,2048]{1,0:T(8,128)(2,1)} %get-tuple-element.12), channel_id=1, source_target_pairs={{0,8},{8,16},{16,24},{24,32},{32,40},{40,48},{48,56},{56,0},{1,9},... | collective-permute-start | bytes 786440 | tf_op jit(solution)/shard_map/ppermute | solution.py:431
  135.4 6.0 %collective-permute-start.1 = (bf16[64,2048]{1,0:T(8,128)(2,1)}, bf16[64,2048]{1,0:T(8,128)(2,1)S(1)}, u32[]{:S(2)}, u32[]{:S(2)}) collective-permute-start(bf16[64,2048]{1,0:T(8,128)(2,1)} %get-tuple-element.13), channel_id=1, source_target_pairs={{8,0},{16,8},{24,16},{32,24},{40,32},{48,40},{56,48},{0,56},{9,1},... | collective-permute-start | bytes 786440 | tf_op jit(solution)/shard_map/ppermute | solution.py:432
Sparse Core Ops, SparseCore 0:
  62.4 88.8 reduce-scatter.1

commit v2 on v1

--- a/solution.py
+++ b/solution.py
@@ -38,9 +38,20 @@
     )
 
 
-def slot_of_row(experts, block, tokens):
-    one = lax.broadcasted_iota(jnp.int32, (block, tokens), 0).astype(jnp.float32)
-    return jnp.concatenate([one] * experts, axis=0)
+def split(cap):
+    main = cap // 8 * 8
+    return main, cap - main
+
+
+def slots_of_rows(experts, cap, tokens):
+    main, tail = split(cap)
+    row = lax.broadcasted_iota(jnp.int32, (2 * cap, tokens), 0)
+    in_first = row < 2 * main + tail
+    first = jnp.where(row < main, row, jnp.where((row >= 2 * main) & in_first, row - main, -1))
+    second = jnp.where(
+        (row >= main) & (row < 2 * main), row - main, jnp.where(in_first, -1, row - main - tail)
+    )
+    return [jnp.concatenate([one.astype(jnp.float32)] * experts, axis=0) for one in (first, second)]
 
 
 def onehot(mask):
@@ -94,9 +105,8 @@
     block = 2 * cap
     picks, member, before = slot_table(ids, experts)
     rows = spread(jnp.where(member, before, NOWHERE), block)
-    slot = slot_of_row(experts, block, tokens)
-    hit_x = rows == slot
-    hit_g = rows + cap == slot
+    first, second = slots_of_rows(experts, cap, tokens)
+    hit_x, hit_g = rows == first, rows == second
     gate = spread(jnp.where(picks[0], gates_ref[0:1, :], gates_ref[1:2, :]), block)
     scale = jnp.sum(
         jnp.where(hit_x, 1.0, 0.0) + jnp.where(hit_g, gate, 0.0), axis=1, keepdims=True
@@ -125,8 +135,8 @@
     half = act_ref.shape[1] // 2
     _, member, before = slot_table(ids, experts)
     rows = spread(jnp.where(member, before, NOWHERE), block)
-    slot = slot_of_row(experts, block, tokens)
-    place_low, place_high = onehot(rows == slot), onehot(rows + cap == slot)
+    first, second = slots_of_rows(experts, cap, tokens)
+    place_low, place_high = onehot(rows == first), onehot(rows == second)
     factor = row_factor(act_ref)
     stores = []
     for at in range(0, half, CHUNK):
@@ -144,34 +154,50 @@
     wait_all(stores)
 
 
-def first_rows(shape, cap):
+def sorted_rows(blocks, cap):
+    main, tail = split(cap)
+    block, whole, short = 2 * cap, blocks * main, 2 * tail
+    firsts = [(pl.ds(i * block, main), pl.ds(i * main, main)) for i in range(blocks)]
+    seconds = [(pl.ds(i * block + main, main), pl.ds(i * main, main)) for i in range(blocks)]
+    tails = [
+        (pl.ds(i * block + 2 * main, short), pl.ds(whole + i * short, short)) for i in range(blocks)
+    ]
+    return firsts, seconds, tails
+
+
+def first_rows(shape, whole, tail):
     row = lax.broadcasted_iota(jnp.int32, shape, 0)
-    return lax.rem(row, 2 * cap) < cap
-
-
-def expert_bwd(cap, scale, recv_hbm, gate_hbm, up_hbm, down_hbm, right_hbm, partial_hbm, recv_ref, right_ref, gate_ref, up_ref, down_ref, pre_g, pre_u, grad, out_ref, sems, out_sems):
+    return (row < whole) | (lax.rem(row - whole + 2 * tail, 2 * tail) < tail)
+
+
+def shift_tail(value, whole, by):
+    short = value.shape[0] - whole
+    return jnp.concatenate([value[:whole], pltpu.roll(value[whole:], by % short, 0)], axis=0)
+
+
+def expert_bwd(blocks, cap, scale, recv_hbm, gate_hbm, up_hbm, down_hbm, right_hbm, partial_hbm, x_ref, g_ref, right_ref, hid_ref, gate_ref, up_ref, down_ref, pre_g, pre_u, grad, out_ref, sems, out_sems):
     hid = gate_ref.shape[1]
-    slots = recv_ref.shape[0]
+    main, tail = split(cap)
+    whole = blocks * main
+    firsts, seconds, tails = sorted_rows(blocks, cap)
     copies = start_all(
-        [
-            (recv_hbm, recv_ref),
-            (down_hbm, down_ref),
-            (gate_hbm, gate_ref),
-            (up_hbm, up_ref),
-        ],
+        [(recv_hbm.at[source, :], g_ref.at[target, :]) for source, target in seconds + tails]
+        + [(down_hbm, down_ref)]
+        + [(recv_hbm.at[source, :], x_ref.at[target, :]) for source, target in firsts + tails]
+        + [(gate_hbm, gate_ref), (up_hbm, up_ref)],
         sems,
     )
-    wait_all(copies[:2])
-    grad[...] = matmul(recv_ref[...], down_ref[...], CONTRACT_LAST)
-    copies[2].wait()
-    pre_g[...] = matmul(recv_ref[...], gate_ref[...])
-    copies[3].wait()
-    pre_u[...] = matmul(recv_ref[...], up_ref[...])
+    wait_all(copies[: 2 * blocks + 1])
+    grad[...] = matmul(g_ref[...], down_ref[...], CONTRACT_LAST)
+    wait_all(copies[2 * blocks + 1 : 4 * blocks + 2])
+    pre_g[...] = matmul(x_ref[...], gate_ref[...])
+    wait_all(copies[4 * blocks + 2 :])
+    pre_u[...] = matmul(x_ref[...], up_ref[...])
     for at in range(0, hid, 128):
         cols = slice(at, at + 128)
         gate, up = pre_g[:, cols], pre_u[:, cols]
-        hidden_grad = pltpu.roll(grad[:, cols], slots - cap, 0)
-        first = first_rows(gate.shape, cap)
+        hidden_grad = shift_tail(grad[:, cols], whole, -tail)
+        first = first_rows(gate.shape, whole, tail)
         sig = 1.0 / (1.0 + jnp.exp(-gate))
         silu = gate * sig
         zero = jnp.zeros_like(gate)
@@ -180,8 +206,8 @@
         right_ref[:, hid + at : hid + at + 128] = jnp.where(
             first, hidden_grad * silu, zero
         ).astype(jnp.bfloat16)
-        hidden = pltpu.roll(jnp.where(first, silu * up, zero), cap, 0)
-        right_ref[:, 2 * hid + at : 2 * hid + at + 128] = hidden.astype(jnp.bfloat16)
+        hidden = shift_tail(jnp.where(first, silu * up, zero), whole, tail)
+        hid_ref[:, cols] = hidden.astype(jnp.bfloat16)
     kept = pltpu.make_async_copy(right_ref, right_hbm, out_sems.at[2])
     kept.start()
     rows = out_ref.shape[1]
@@ -190,8 +216,11 @@
         slot = i % 2
         if i >= 2:
             stores[i - 2].wait()
-        left = recv_ref[:, i * rows : (i + 1) * rows]
-        out_ref[slot] = (matmul(left, right_ref[...], CONTRACT_FIRST) * scale).astype(jnp.bfloat16)
+        span = slice(i * rows, (i + 1) * rows)
+        wide = matmul(x_ref[:, span], right_ref[...], CONTRACT_FIRST) * scale
+        out_ref[slot, :, : 2 * hid] = wide.astype(jnp.bfloat16)
+        wide = matmul(g_ref[:, span], hid_ref[...], CONTRACT_FIRST) * scale
+        out_ref[slot, :, 2 * hid :] = wide.astype(jnp.bfloat16)
         store = pltpu.make_async_copy(
             out_ref.at[slot], partial_hbm.at[pl.ds(i * rows, rows), :], out_sems.at[slot]
         )
@@ -200,41 +229,78 @@
     wait_all(stores[-2:] + [kept])
 
 
-def expert_fwd(cap, recv_hbm, right_hbm, gate_hbm, up_hbm, down_hbm, out_hbm, recv_ref, right_ref, out_ref, gate_ref, up_ref, down_ref, low_g, low_u, high_g, high_u, hid_ref, sems, out_sems):
+def expert_fwd(blocks, cap, recv_hbm, right_hbm, gate_hbm, up_hbm, down_hbm, out_hbm, rows_ref, right_ref, one_ref, two_ref, gate_ref, up_ref, down_ref, low_g, low_u, high_g, high_u, hid_ref, sems, out_sems):
     hid = gate_ref.shape[1]
-    slots, half = recv_ref.shape
+    main, tail = split(cap)
+    whole = blocks * main
+    half = recv_hbm.shape[1]
+    firsts, seconds, tails = sorted_rows(blocks, cap)
+    low_cols, high_cols = pl.ds(0, half), pl.ds(half, half)
     copies = start_all(
-        [
-            (recv_hbm, recv_ref),
-            (gate_hbm, gate_ref),
-            (up_hbm, up_ref),
-            (right_hbm, right_ref),
-            (down_hbm, down_ref),
-        ],
+        [(recv_hbm.at[source, :], rows_ref.at[target, low_cols]) for source, target in firsts + tails]
+        + [(recv_hbm.at[source, :], rows_ref.at[target, high_cols]) for source, target in seconds + tails]
+        + [(gate_hbm, gate_ref), (up_hbm, up_ref), (right_hbm, right_ref), (down_hbm, down_ref)],
         sems,
     )
-    wait_all(copies[:2])
-    low_g[...] = matmul(recv_ref[...], gate_ref[:half, :])
-    high_g[...] = matmul(recv_ref[...], gate_ref[half:, :])
-    copies[2].wait()
-    low_u[...] = matmul(recv_ref[...], up_ref[:half, :])
-    high_u[...] = matmul(recv_ref[...], up_ref[half:, :])
+    wait_all(copies[:-3])
+    low_g[...] = matmul(rows_ref[:, :half], gate_ref[:half, :])
+    high_g[...] = matmul(rows_ref[:, half:], gate_ref[half:, :])
+    copies[-3].wait()
+    low_u[...] = matmul(rows_ref[:, :half], up_ref[:half, :])
+    high_u[...] = matmul(rows_ref[:, half:], up_ref[half:, :])
     for at in range(0, hid, 128):
         cols = slice(at, at + 128)
-        gate = low_g[:, cols] + pltpu.roll(high_g[:, cols], slots - cap, 0)
-        up = low_u[:, cols] + pltpu.roll(high_u[:, cols], slots - cap, 0)
+        gate = low_g[:, cols] + shift_tail(high_g[:, cols], whole, -tail)
+        up = low_u[:, cols] + shift_tail(high_u[:, cols], whole, -tail)
         hidden = gate / (1.0 + jnp.exp(-gate)) * up
-        hidden = jnp.where(first_rows(gate.shape, cap), hidden, jnp.zeros_like(hidden))
-        hid_ref[:, cols] = pltpu.roll(hidden, cap, 0).astype(jnp.bfloat16)
-    wait_all(copies[3:])
-    stores = []
-    for at in range(0, out_ref.shape[1], CHUNK):
-        cols = slice(at, at + CHUNK)
-        total = matmul(hid_ref[...], down_ref[:, cols])
-        total = total + matmul(right_ref[:, :hid], gate_ref[cols, :], CONTRACT_LAST)
-        total = total + matmul(right_ref[:, hid : 2 * hid], up_ref[cols, :], CONTRACT_LAST)
-        out_ref[:, cols] = total.astype(jnp.bfloat16)
-        store_columns(stores, out_ref, out_hbm, at, CHUNK, out_sems)
+        hidden = jnp.where(first_rows(gate.shape, whole, tail), hidden, jnp.zeros_like(hidden))
+        hid_ref[:, cols] = shift_tail(hidden, whole, tail).astype(jnp.bfloat16)
+    wait_all(copies[-2:])
+    stores = []
+    width = out_hbm.shape[1]
+    span = width // 2
+    for start in range(0, width, span):
+        for at in range(start, start + span, CHUNK):
+            cols = slice(at, at + CHUNK)
+            one = matmul(right_ref[:, :hid], gate_ref[cols, :], CONTRACT_LAST)
+            one = one + matmul(right_ref[:, hid:], up_ref[cols, :], CONTRACT_LAST)
+            two = matmul(hid_ref[...], down_ref[:, cols])
+            one_ref[:whole, cols] = one[:whole].astype(jnp.bfloat16)
+            one_ref[whole:, cols] = (one[whole:] + two[whole:]).astype(jnp.bfloat16)
+            two_ref[:, cols] = two[:whole].astype(jnp.bfloat16)
+        part = pl.ds(start, span)
+        for source, targets in ((one_ref, firsts), (two_ref, seconds), (one_ref, tails)):
+            for target, rows in targets:
+                copy = pltpu.make_async_copy(
+                    source.at[rows, part], out_hbm.at[target, part], out_sems.at[len(stores)]
+                )
+                copy.start()
+                stores.append(copy)
+    wait_all(stores)
+
+
+def widen(narrow_hbm, wide_hbm, narrow_ref, wide_ref, sems):
+    parts = narrow_ref.shape[0] // 32
+    spans = [pl.ds(i * 32, 32) for i in range(parts)]
+    copies = start_all([(narrow_hbm.at[span, :], narrow_ref.at[span, :]) for span in spans], sems)
+    stores = []
+    for i, span in enumerate(spans):
+        copies[i].wait()
+        wide_ref[span, :] = narrow_ref[span, :].astype(jnp.float32)
+        store = pltpu.make_async_copy(wide_ref.at[span, :], wide_hbm.at[span, :], sems.at[parts + i])
+        store.start()
+        stores.append(store)
+    wait_all(stores)
+
+
+def settle(one_hbm, two_hbm, one_out, two_out, one_ref, two_ref, sems):
+    copies = start_all([(one_hbm, one_ref), (two_hbm, two_ref)], sems)
+    stores = []
+    for i, (held, target) in enumerate(((one_ref, one_out), (two_ref, two_out))):
+        copies[i].wait()
+        store = pltpu.make_async_copy(held, target, sems.at[2 + i])
+        store.start()
+        stores.append(store)
     wait_all(stores)
 
 
@@ -263,12 +329,12 @@
     wait_all(copies[:3])
     tokens, width = act_ref.shape
     block = 2 * cap
-    slot = slot_of_row(experts, block, tokens)
+    first, second = slots_of_rows(experts, cap, tokens)
     picks, _, before = slot_table(fwd_ids_ref[...], experts)
-    chosen = [onehot(spread(jnp.where(pick, before, NOWHERE), block) + cap == slot) for pick in picks]
+    chosen = [onehot(spread(jnp.where(pick, before, NOWHERE), block) == second) for pick in picks]
     gates = [as_column(gates_ref[k : k + 1, :]) for k in range(len(picks))]
     _, member, before = slot_table(bwd_ids_ref[...], experts)
-    both = onehot(spread(jnp.where(member, before, NOWHERE), block) == slot)
+    both = onehot(spread(jnp.where(member, before, NOWHERE), block) == first)
     wait_all(copies[3:])
     factor = row_factor(saved_ref)
     inner = jnp.zeros((tokens, 1), jnp.float32)
@@ -343,7 +409,11 @@
     gain_buf = pltpu.VMEM((1, width), jnp.float32)
     slots_buf = pltpu.VMEM((slots, width), jnp.bfloat16)
     half_buf = pltpu.VMEM((slots, width // 2), jnp.bfloat16)
-    right_buf = pltpu.VMEM((slots, 3 * hid), jnp.bfloat16)
+    main, tail = split(cap)
+    rows = experts * (main + 2 * tail)
+    sorted_buf = pltpu.VMEM((rows, width), jnp.bfloat16)
+    right_buf = pltpu.VMEM((rows, 2 * hid), jnp.bfloat16)
+    hid_buf = pltpu.VMEM((rows, hid), jnp.bfloat16)
     chunks = width // CHUNK
     dma = lambda count: pltpu.SemaphoreType.DMA((count,))
     weight_bufs = [
@@ -373,23 +443,21 @@
         cost_estimate=cost(2 * slots * tokens * width, small + big // 2),
         name="pack_fwd",
     )(ids_fwd, here, norm_gain)
-    send_fwd, recv_bwd = lax.optimization_barrier((send_fwd, recv_bwd))
-    recv_fwd = exchange(send_fwd, experts)
 
     right, partial = pl.pallas_call(
-        functools.partial(expert_bwd, cap, 1.0 / replicas),
+        functools.partial(expert_bwd, experts, cap, 1.0 / replicas),
         out_shape=(
-            jax.ShapeDtypeStruct((slots, 3 * hid), jnp.bfloat16),
+            jax.ShapeDtypeStruct((rows, 2 * hid), jnp.bfloat16),
             jax.ShapeDtypeStruct((width, 3 * hid), jnp.bfloat16),
         ),
         in_specs=[HBM] * 4,
         out_specs=(HBM, HBM),
-        scratch_shapes=[slots_buf, right_buf]
+        scratch_shapes=[sorted_buf, sorted_buf, right_buf, hid_buf]
         + weight_bufs
-        + [pltpu.VMEM((slots, hid), jnp.float32)] * 3
+        + [pltpu.VMEM((rows, hid), jnp.float32)] * 3
         + [
             pltpu.VMEM((2, 256, 3 * hid), jnp.bfloat16),
-            dma(4),
+            dma(4 * experts + 3),
             dma(3),
         ],
         compiler_params=PARAMS,
@@ -397,16 +465,33 @@
         name="expert_bwd",
     )(recv_bwd, weight_gate, weight_up, weight_down)
     summed = lax.psum_scatter(partial, "dp", scatter_dimension=0, tiled=True)
+    total = pl.pallas_call(
+        widen,
+        out_shape=jax.ShapeDtypeStruct(summed.shape, jnp.float32),
+        in_specs=[HBM],
+        out_specs=HBM,
+        scratch_shapes=[
+            pltpu.VMEM(summed.shape, jnp.bfloat16),
+            pltpu.VMEM(summed.shape, jnp.float32),
+            dma(2 * (summed.shape[0] // 32)),
+        ],
+        compiler_params=PARAMS,
+        cost_estimate=cost(0, 6 * summed.size),
+        name="widen",
+    )(summed)
+
+    send_fwd, right = lax.optimization_barrier((send_fwd, right))
+    recv_fwd = exchange(send_fwd, experts)
 
     back = pl.pallas_call(
-        functools.partial(expert_fwd, cap),
+        functools.partial(expert_fwd, experts, cap),
         out_shape=jax.ShapeDtypeStruct((slots, width), jnp.bfloat16),
         in_specs=[HBM] * 5,
         out_specs=HBM,
-        scratch_shapes=[half_buf, right_buf, slots_buf]
+        scratch_shapes=[sorted_buf, right_buf, sorted_buf, pltpu.VMEM((main * experts, width), jnp.bfloat16)]
         + weight_bufs
-        + [pltpu.VMEM((slots, hid), jnp.float32)] * 4
-        + [pltpu.VMEM((slots, hid), jnp.bfloat16), dma(5), dma(chunks)],
+        + [pltpu.VMEM((rows, hid), jnp.float32)] * 4
+        + [hid_buf, dma(4 * experts + 4), dma(6 * experts)],
         compiler_params=PARAMS,
         cost_estimate=cost(10 * slots * width * hid, 2 * big + weight_bytes),
         name="expert_fwd",
@@ -430,7 +515,20 @@
     ring = [(i, (i + 1) % sections) for i in range(sections)]
     act_out = lax.ppermute(layer_out, "section", ring)
     grad_out = lax.ppermute(input_grad, "section", [(target, source) for source, target in ring])
-    return (act_out[None], grad_out[None], summed.astype(jnp.float32)[None, None])
+    act_out, grad_out = pl.pallas_call(
+        settle,
+        out_shape=(
+            jax.ShapeDtypeStruct(act_out.shape, act_out.dtype),
+            jax.ShapeDtypeStruct(grad_out.shape, grad_out.dtype),
+        ),
+        in_specs=[HBM, HBM],
+        out_specs=(HBM, HBM),
+        scratch_shapes=[rows_buf, rows_buf, dma(4)],
+        compiler_params=PARAMS,
+        cost_estimate=cost(0, 4 * small),
+        name="settle",
+    )(act_out, grad_out)
+    return (act_out[None], grad_out[None], total[None, None])
 
 
 def solution(mesh):

time: 162 us -> 159 us (0.981)
  the two profiles are of different devices: /device:TPU:2 before, /device:TPU:18 now
where the time goes in v2:
time: 159 us
  blocking collectives  98.1 us (62%)
  Pallas kernels  27.9 us (18%)
  waiting for transfers between devices  16.6 us (10%)
  between operations  14.1 us (9%)
  starting transfers between devices  1.79 us (1%)
    all_to_all x3, blocking collectives, exchange(): lax.all_to_all(blocks, 'expert', split_axis=0, concat_axis=0, tiled=True)  98.1 us
    reduce_scatter x1, waiting for transfers between devices, shards(): summed = lax.psum_scatter(partial, 'dp', scatter_dimension=0, tiled=True)  12.3 us
    pallas_call x1, Pallas kernels, shards(): pl.pallas_call(functools.partial(expert_bwd, experts, cap, 1.0 / replicas...  9.51 us
    pallas_call x1, Pallas kernels, shards(): pl.pallas_call(functools.partial(expert_fwd, experts, cap), out_shape=jax...  6.23 us
    ppermute x1, waiting for transfers between devices, shards(): act_out = lax.ppermute(layer_out, 'section', ring)  4.37 us
    pallas_call x1, Pallas kernels, shards(): pl.pallas_call(functools.partial(combine, experts, cap), out_shape=(jax.S...  3.45 us
  transfers between devices with their start and end apart: 3, of which 2 were waited for; matrix products, arithmetic and copies ran while one was open for 0% of the time, Pallas kernels for 9%

profile of v2, /device:TPU:18, one launch (start us, length us, event | category | flops | bytes accessed | tf_op | source)
XLA Modules:
  0.0 158.6 jit_solution(18133512091752167961)
XLA Ops:
  7.2 0.0 reduce-scatter.2.cloned.1.call-start
  7.2 2.8 %pack_bwd.1 = bf16[320,2048]{1,0:T(8,128)(2,1)} custom-call(s32[2,64]{1,0:T(2,128)} %bitcast.40, f32[2,64]{1,0:T(2,128)} %bitcast.44, bf16[64,2048]{1,0:T(8,128)(2,1)} %bitcast.34, bf16[64,2048]{1,0:T(8,128)(2,1)} %bitcast.36, f32[1,2048]{1,0:T(1,128)} %gain_hbm.5), custom_call_target="tpu_custom_call" | custom-call | flops 167772160 | bytes 1835008 | tf_op jit(solution)/shard_map/pack_bwd/pallas_call | solution.py:425
  10.0 39.0 %all_to_all.15 = bf16[8,40,2048]{2,1,0:T(8,128)(2,1)} all-to-all(bf16[8,40,2048]{2,1,0:T(8,128)(2,1)} %bitcast.28), channel_id=1, replica_groups=mesh['dp'=16,'section'=8,'expert'=8] {'expert'}, dimensions={0} | all-to-all | bytes 2621440 | tf_op jit(solution)/shard_map/all_to_all | solution.py:374
  49.0 9.5 %expert_bwd.1 = (bf16[192,768]{1,0:T(8,128)(2,1)}, bf16[2048,1152]{1,0:T(8,128)(2,1)}) custom-call(bf16[320,2048]{1,0:T(8,128)(2,1)} %bitcast.30, bf16[2048,384]{1,0:T(8,128)(2,1)} %bitcast.46, bf16[2048,384]{1,0:T(8,128)(2,1)} %bitcast.48, bf16[384,2048]{1,0:T(8,128)(2,1)} %bitcast.50), custom_call_target="tpu_custom_call" | custom-call | flops 3019898880 | bytes 10747904 | tf_op jit(solution)/shard_map/expert_bwd/pallas_call | solution.py:447
  58.5 0.0 reduce-scatter.2.cloned.1.call-update
  58.5 2.4 %pack_fwd.1 = bf16[320,1024]{1,0:T(8,128)(2,1)} custom-call(s32[2,64]{1,0:T(2,128)} %bitcast.42, bf16[64,2048]{1,0:T(8,128)(2,1)} %bitcast.32, f32[1,2048]{1,0:T(1,128)} %gain_hbm.5), custom_call_target="tpu_custom_call" | custom-call | flops 83886080 | bytes 917504 | tf_op jit(solution)/shard_map/pack_fwd/pallas_call | solution.py:436
  60.9 23.2 %all_to_all.16 = bf16[8,40,1024]{2,1,0:T(8,128)(2,1)} all-to-all(bf16[8,40,1024]{2,1,0:T(8,128)(2,1)} %bitcast.29), channel_id=1, replica_groups=mesh['dp'=16,'section'=8,'expert'=8] {'expert'}, dimensions={0} | all-to-all | bytes 1310720 | tf_op jit(solution)/shard_map/all_to_all | solution.py:374
  84.1 6.2 %expert_fwd.1 = bf16[320,2048]{1,0:T(8,128)(2,1)} custom-call(bf16[320,1024]{1,0:T(8,128)(2,1)} %bitcast.38, bf16[192,768]{1,0:T(8,128)(2,1)} %get-tuple-element.13.right_hbm, bf16[2048,384]{1,0:T(8,128)(2,1)} %bitcast.47, bf16[2048,384]{1,0:T(8,128)(2,1)} %bitcast.49, bf16[384,2048]{1,0:T(8,128)(2,1)} %bitcast.51), custom_call_target="tpu_custom_call" | custom-call | flops 2516582400 | bytes 7340032 | tf_op jit(solution)/shard_map/expert_fwd/pallas_call | solution.py:486
  90.3 36.0 %all_to_all.17 = bf16[8,40,2048]{2,1,0:T(8,128)(2,1)} all-to-all(bf16[8,40,2048]{2,1,0:T(8,128)(2,1)} %bitcast.31), channel_id=1, replica_groups=mesh['dp'=16,'section'=8,'expert'=8] {'expert'}, dimensions={0} | all-to-all | bytes 2621440 | tf_op jit(solution)/shard_map/all_to_all | solution.py:374
  126.3 3.5 %combine.1 = (bf16[64,2048]{1,0:T(8,128)(2,1)}, bf16[64,2048]{1,0:T(8,128)(2,1)}) custom-call(bf16[320,2048]{1,0:T(8,128)(2,1)} %bitcast.27, s32[2,64]{1,0:T(2,128)} %bitcast.43, s32[2,64]{1,0:T(2,128)} %bitcast.41, f32[2,64]{1,0:T(2,128)} %bitcast.45, bf16[64,2048]{1,0:T(8,128)(2,1)} %bitcast.33, bf16[64,2048]{1,0:T(8,128)(2,1)} %bitcast.35, ...), custom_call_target="tpu_custom_call" | custom-call | flops 251658240 | bytes 2621440 | tf_op jit(solution)/shard_map/combine/pallas_call | solution.py:501
  129.8 0.0 collective-permute-start
  129.8 1.7 %collective-permute-start.1 = (bf16[64,2048]{1,0:T(8,128)(2,1)}, bf16[64,2048]{1,0:T(8,128)(2,1)}, u32[]{:S(2)}, u32[]{:S(2)}) collective-permute-start(bf16[64,2048]{1,0:T(8,128)(2,1)} %get-tuple-element.15), channel_id=1, source_target_pairs={{8,0},{16,8},{24,16},{32,24},{40,32},{48,40},{56,48},{0,56},{9,1},... | collective-permute-start | bytes 786440 | tf_op jit(solution)/shard_map/ppermute | solution.py:517
  131.6 4.4 %collective-permute-done.one_hbm = bf16[64,2048]{1,0:T(8,128)(2,1)} collective-permute-done((bf16[64,2048]{1,0:T(8,128)(2,1)}, bf16[64,2048]{1,0:T(8,128)(2,1)}, u32[]{:S(2)}, u32[]{:S(2)}) %collective-permute-start) | collective-permute-done | bytes 262176 | tf_op jit(solution)/shard_map/ppermute | solution.py:516
  135.9 0.0 collective-permute-done.1.two_hbm
  135.9 1.8 %settle.1 = (bf16[64,2048]{1,0:T(8,128)(2,1)}, bf16[64,2048]{1,0:T(8,128)(2,1)}) custom-call(bf16[64,2048]{1,0:T(8,128)(2,1)} %collective-permute-done.one_hbm, bf16[64,2048]{1,0:T(8,128)(2,1)} %collective-permute-done.1.two_hbm), custom_call_target="tpu_custom_call" | custom-call | bytes 1048576 | tf_op jit(solution)/shard_map/settle/pallas_call | solution.py:518
  137.7 12.3 %reduce-scatter.2.cloned.1.call-done.narrow_hbm = bf16[128,1152]{1,0:T(8,128)(2,1)} async-done(((bf16[2048,1152]{1,0:T(8,128)(2,1)}), bf16[128,1152]{1,0:T(8,128)(2,1)}) %reduce-scatter.2.cloned.1.call-update) | async-done | bytes 294928 | tf_op jit(solution)/shard_map/reduce_scatter | solution.py:467
  150.0 1.8 %widen.1 = f32[128,1152]{1,0:T(8,128)} custom-call(bf16[128,1152]{1,0:T(8,128)(2,1)} %reduce-scatter.2.cloned.1.call-done.narrow_hbm), custom_call_target="tpu_custom_call" | custom-call | bytes 884736 | tf_op jit(solution)/shard_map/widen/pallas_call | solution.py:468
Async XLA Ops:
  7.2 142.8 %reduce-scatter.2.cloned.1.call-start = ((), (), s32[]{:S(2)}) async-start(), calls=%async_computation.4 | async-start | bytes 5013504 | tf_op jit(solution)/shard_map/reduce_scatter | solution.py:467
  129.8 6.1 %collective-permute-start = (bf16[64,2048]{1,0:T(8,128)(2,1)}, bf16[64,2048]{1,0:T(8,128)(2,1)}, u32[]{:S(2)}, u32[]{:S(2)}) collective-permute-start(bf16[64,2048]{1,0:T(8,128)(2,1)} %get-tuple-element.14), channel_id=1, source_target_pairs={{0,8},{8,16},{16,24},{24,32},{32,40},{40,48},{48,56},{56,0},{1,9},... | collective-permute-start | bytes 786440 | tf_op jit(solution)/shard_map/ppermute | solution.py:516
  129.8 6.1 %collective-permute-start.1 = (bf16[64,2048]{1,0:T(8,128)(2,1)}, bf16[64,2048]{1,0:T(8,128)(2,1)}, u32[]{:S(2)}, u32[]{:S(2)}) collective-permute-start(bf16[64,2048]{1,0:T(8,128)(2,1)} %get-tuple-element.15), channel_id=1, source_target_pairs={{8,0},{16,8},{24,16},{32,24},{40,32},{48,40},{56,48},{0,56},{9,1},... | collective-permute-start | bytes 786440 | tf_op jit(solution)/shard_map/ppermute | solution.py:517
Sparse Core Ops, SparseCore 0:
  58.6 91.3 reduce-scatter.1

commit v3 on v2

--- a/solution.py
+++ b/solution.py
@@ -175,8 +175,8 @@
     return jnp.concatenate([value[:whole], pltpu.roll(value[whole:], by % short, 0)], axis=0)
 
 
-def expert_bwd(blocks, cap, scale, recv_hbm, gate_hbm, up_hbm, down_hbm, right_hbm, partial_hbm, x_ref, g_ref, right_ref, hid_ref, gate_ref, up_ref, down_ref, pre_g, pre_u, grad, out_ref, sems, out_sems):
-    hid = gate_ref.shape[1]
+def expert_bwd(blocks, cap, scale, recv_hbm, gate_hbm, up_hbm, down_hbm, right_hbm, partial_hbm, x_ref, g_ref, right_ref, hid_ref, pair_ref, down_ref, pre, grad, out_ref, sems, out_sems):
+    hid = down_ref.shape[0]
     main, tail = split(cap)
     whole = blocks * main
     firsts, seconds, tails = sorted_rows(blocks, cap)
@@ -184,18 +184,16 @@
         [(recv_hbm.at[source, :], g_ref.at[target, :]) for source, target in seconds + tails]
         + [(down_hbm, down_ref)]
         + [(recv_hbm.at[source, :], x_ref.at[target, :]) for source, target in firsts + tails]
-        + [(gate_hbm, gate_ref), (up_hbm, up_ref)],
+        + [(gate_hbm, pair_ref.at[:, pl.ds(0, hid)]), (up_hbm, pair_ref.at[:, pl.ds(hid, hid)])],
         sems,
     )
     wait_all(copies[: 2 * blocks + 1])
     grad[...] = matmul(g_ref[...], down_ref[...], CONTRACT_LAST)
-    wait_all(copies[2 * blocks + 1 : 4 * blocks + 2])
-    pre_g[...] = matmul(x_ref[...], gate_ref[...])
-    wait_all(copies[4 * blocks + 2 :])
-    pre_u[...] = matmul(x_ref[...], up_ref[...])
+    wait_all(copies[2 * blocks + 1 :])
+    pre[...] = matmul(x_ref[...], pair_ref[...])
     for at in range(0, hid, 128):
         cols = slice(at, at + 128)
-        gate, up = pre_g[:, cols], pre_u[:, cols]
+        gate, up = pre[:, cols], pre[:, hid + at : hid + at + 128]
         hidden_grad = shift_tail(grad[:, cols], whole, -tail)
         first = first_rows(gate.shape, whole, tail)
         sig = 1.0 / (1.0 + jnp.exp(-gate))
@@ -208,29 +206,29 @@
         ).astype(jnp.bfloat16)
         hidden = shift_tail(jnp.where(first, silu * up, zero), whole, tail)
         hid_ref[:, cols] = hidden.astype(jnp.bfloat16)
-    kept = pltpu.make_async_copy(right_ref, right_hbm, out_sems.at[2])
+    kept = pltpu.make_async_copy(right_ref, right_hbm, out_sems.at[3])
     kept.start()
-    rows = out_ref.shape[1]
-    stores = []
-    for i in range(partial_hbm.shape[0] // rows):
-        slot = i % 2
-        if i >= 2:
-            stores[i - 2].wait()
-        span = slice(i * rows, (i + 1) * rows)
+    stores = []
+    at, width = 0, out_ref.shape[0]
+    while at < width:
+        rows = min(1024 if at == 0 else 512, width - at)
+        span = slice(at, at + rows)
         wide = matmul(x_ref[:, span], right_ref[...], CONTRACT_FIRST) * scale
-        out_ref[slot, :, : 2 * hid] = wide.astype(jnp.bfloat16)
+        out_ref[span, : 2 * hid] = wide.astype(jnp.bfloat16)
         wide = matmul(g_ref[:, span], hid_ref[...], CONTRACT_FIRST) * scale
-        out_ref[slot, :, 2 * hid :] = wide.astype(jnp.bfloat16)
+        out_ref[span, 2 * hid :] = wide.astype(jnp.bfloat16)
+        part = pl.ds(at, rows)
         store = pltpu.make_async_copy(
-            out_ref.at[slot], partial_hbm.at[pl.ds(i * rows, rows), :], out_sems.at[slot]
+            out_ref.at[part, :], partial_hbm.at[part, :], out_sems.at[len(stores)]
         )
         store.start()
         stores.append(store)
-    wait_all(stores[-2:] + [kept])
-
-
-def expert_fwd(blocks, cap, recv_hbm, right_hbm, gate_hbm, up_hbm, down_hbm, out_hbm, rows_ref, right_ref, one_ref, two_ref, gate_ref, up_ref, down_ref, low_g, low_u, high_g, high_u, hid_ref, sems, out_sems):
-    hid = gate_ref.shape[1]
+        at += rows
+    wait_all(stores + [kept])
+
+
+def expert_fwd(blocks, cap, recv_hbm, right_hbm, gate_hbm, up_hbm, down_hbm, out_hbm, rows_ref, right_ref, one_ref, two_ref, pair_ref, down_ref, low, high, hid_ref, sems, out_sems):
+    hid = down_ref.shape[0]
     main, tail = split(cap)
     whole = blocks * main
     half = recv_hbm.shape[1]
@@ -239,19 +237,18 @@
     copies = start_all(
         [(recv_hbm.at[source, :], rows_ref.at[target, low_cols]) for source, target in firsts + tails]
         + [(recv_hbm.at[source, :], rows_ref.at[target, high_cols]) for source, target in seconds + tails]
-        + [(gate_hbm, gate_ref), (up_hbm, up_ref), (right_hbm, right_ref), (down_hbm, down_ref)],
+        + [(gate_hbm, pair_ref.at[:, pl.ds(0, hid)]), (up_hbm, pair_ref.at[:, pl.ds(hid, hid)])]
+        + [(right_hbm, right_ref), (down_hbm, down_ref)],
         sems,
     )
-    wait_all(copies[:-3])
-    low_g[...] = matmul(rows_ref[:, :half], gate_ref[:half, :])
-    high_g[...] = matmul(rows_ref[:, half:], gate_ref[half:, :])
-    copies[-3].wait()
-    low_u[...] = matmul(rows_ref[:, :half], up_ref[:half, :])
-    high_u[...] = matmul(rows_ref[:, half:], up_ref[half:, :])
+    wait_all(copies[:-2])
+    low[...] = matmul(rows_ref[:, :half], pair_ref[:half, :])
+    high[...] = matmul(rows_ref[:, half:], pair_ref[half:, :])
     for at in range(0, hid, 128):
         cols = slice(at, at + 128)
-        gate = low_g[:, cols] + shift_tail(high_g[:, cols], whole, -tail)
-        up = low_u[:, cols] + shift_tail(high_u[:, cols], whole, -tail)
+        others = slice(hid + at, hid + at + 128)
+        gate = low[:, cols] + shift_tail(high[:, cols], whole, -tail)
+        up = low[:, others] + shift_tail(high[:, others], whole, -tail)
         hidden = gate / (1.0 + jnp.exp(-gate)) * up
         hidden = jnp.where(first_rows(gate.shape, whole, tail), hidden, jnp.zeros_like(hidden))
         hid_ref[:, cols] = shift_tail(hidden, whole, tail).astype(jnp.bfloat16)
@@ -262,8 +259,7 @@
     for start in range(0, width, span):
         for at in range(start, start + span, CHUNK):
             cols = slice(at, at + CHUNK)
-            one = matmul(right_ref[:, :hid], gate_ref[cols, :], CONTRACT_LAST)
-            one = one + matmul(right_ref[:, hid:], up_ref[cols, :], CONTRACT_LAST)
+            one = matmul(right_ref[...], pair_ref[cols, :], CONTRACT_LAST)
             two = matmul(hid_ref[...], down_ref[:, cols])
             one_ref[:whole, cols] = one[:whole].astype(jnp.bfloat16)
             one_ref[whole:, cols] = (one[whole:] + two[whole:]).astype(jnp.bfloat16)
@@ -417,8 +413,7 @@
     chunks = width // CHUNK
     dma = lambda count: pltpu.SemaphoreType.DMA((count,))
     weight_bufs = [
-        pltpu.VMEM((width, hid), jnp.bfloat16),
-        pltpu.VMEM((width, hid), jnp.bfloat16),
+        pltpu.VMEM((width, 2 * hid), jnp.bfloat16),
         pltpu.VMEM((hid, width), jnp.bfloat16),
     ]
 
@@ -454,11 +449,11 @@
         out_specs=(HBM, HBM),
         scratch_shapes=[sorted_buf, sorted_buf, right_buf, hid_buf]
         + weight_bufs
-        + [pltpu.VMEM((rows, hid), jnp.float32)] * 3
+        + [pltpu.VMEM((rows, 2 * hid), jnp.float32), pltpu.VMEM((rows, hid), jnp.float32)]
         + [
-            pltpu.VMEM((2, 256, 3 * hid), jnp.bfloat16),
+            pltpu.VMEM((width, 3 * hid), jnp.bfloat16),
             dma(4 * experts + 3),
-            dma(3),
+            dma(4),
         ],
         compiler_params=PARAMS,
         cost_estimate=cost(12 * slots * width * hid, big + 2 * weight_bytes),
@@ -490,7 +485,7 @@
         out_specs=HBM,
         scratch_shapes=[sorted_buf, right_buf, sorted_buf, pltpu.VMEM((main * experts, width), jnp.bfloat16)]
         + weight_bufs
-        + [pltpu.VMEM((rows, hid), jnp.float32)] * 4
+        + [pltpu.VMEM((rows, 2 * hid), jnp.float32)] * 2
         + [hid_buf, dma(4 * experts + 4), dma(6 * experts)],
         compiler_params=PARAMS,
         cost_estimate=cost(10 * slots * width * hid, 2 * big + weight_bytes),

time: 159 us -> 157 us (0.987)
  the two profiles are of different devices: /device:TPU:18 before, /device:TPU:10 now
where the time goes in v3:
time: 157 us
  blocking collectives  99.5 us (63%)
  Pallas kernels  26.2 us (17%)
  waiting for transfers between devices  14.9 us (9%)
  between operations  14.1 us (9%)
  starting transfers between devices  1.79 us (1%)
    all_to_all x3, blocking collectives, exchange(): lax.all_to_all(blocks, 'expert', split_axis=0, concat_axis=0, tiled=True)  99.5 us
    reduce_scatter x1, waiting for transfers between devices, shards(): summed = lax.psum_scatter(partial, 'dp', scatter_dimension=0, tiled=True)  10.5 us
    pallas_call x1, Pallas kernels, shards(): pl.pallas_call(functools.partial(expert_bwd, experts, cap, 1.0 / replicas...  7.42 us
    pallas_call x1, Pallas kernels, shards(): pl.pallas_call(functools.partial(expert_fwd, experts, cap), out_shape=jax...  6.6 us
    ppermute x1, waiting for transfers between devices, shards(): act_out = lax.ppermute(layer_out, 'section', ring)  4.37 us
    pallas_call x1, Pallas kernels, shards(): pl.pallas_call(functools.partial(combine, experts, cap), out_shape=(jax.S...  3.45 us
  transfers between devices with their start and end apart: 3, of which 2 were waited for; matrix products, arithmetic and copies ran while one was open for 0% of the time, Pallas kernels for 9%

profile of v3, /device:TPU:10, one launch (start us, length us, event | category | flops | bytes accessed | tf_op | source)
XLA Modules:
  0.0 156.5 jit_solution(18046172882439841592)
XLA Ops:
  7.2 0.0 reduce-scatter.2.cloned.1.call-start
  7.2 2.8 %pack_bwd.1 = bf16[320,2048]{1,0:T(8,128)(2,1)} custom-call(s32[2,64]{1,0:T(2,128)} %bitcast.40, f32[2,64]{1,0:T(2,128)} %bitcast.44, bf16[64,2048]{1,0:T(8,128)(2,1)} %bitcast.34, bf16[64,2048]{1,0:T(8,128)(2,1)} %bitcast.36, f32[1,2048]{1,0:T(1,128)} %gain_hbm.5), custom_call_target="tpu_custom_call" | custom-call | flops 167772160 | bytes 1835008 | tf_op jit(solution)/shard_map/pack_bwd/pallas_call | solution.py:420
  10.0 40.5 %all_to_all.15 = bf16[8,40,2048]{2,1,0:T(8,128)(2,1)} all-to-all(bf16[8,40,2048]{2,1,0:T(8,128)(2,1)} %bitcast.28), channel_id=1, replica_groups=mesh['dp'=16,'section'=8,'expert'=8] {'expert'}, dimensions={0} | all-to-all | bytes 2621440 | tf_op jit(solution)/shard_map/all_to_all | solution.py:370
  50.5 7.4 %expert_bwd.1 = (bf16[192,768]{1,0:T(8,128)(2,1)}, bf16[2048,1152]{1,0:T(8,128)(2,1)}) custom-call(bf16[320,2048]{1,0:T(8,128)(2,1)} %bitcast.30, bf16[2048,384]{1,0:T(8,128)(2,1)} %bitcast.46, bf16[2048,384]{1,0:T(8,128)(2,1)} %bitcast.48, bf16[384,2048]{1,0:T(8,128)(2,1)} %bitcast.50), custom_call_target="tpu_custom_call" | custom-call | flops 3019898880 | bytes 10747904 | tf_op jit(solution)/shard_map/expert_bwd/pallas_call | solution.py:442
  58.0 0.0 reduce-scatter.2.cloned.1.call-update
  58.0 2.4 %pack_fwd.1 = bf16[320,1024]{1,0:T(8,128)(2,1)} custom-call(s32[2,64]{1,0:T(2,128)} %bitcast.42, bf16[64,2048]{1,0:T(8,128)(2,1)} %bitcast.32, f32[1,2048]{1,0:T(1,128)} %gain_hbm.5), custom_call_target="tpu_custom_call" | custom-call | flops 83886080 | bytes 917504 | tf_op jit(solution)/shard_map/pack_fwd/pallas_call | solution.py:431
  60.4 23.1 %all_to_all.16 = bf16[8,40,1024]{2,1,0:T(8,128)(2,1)} all-to-all(bf16[8,40,1024]{2,1,0:T(8,128)(2,1)} %bitcast.29), channel_id=1, replica_groups=mesh['dp'=16,'section'=8,'expert'=8] {'expert'}, dimensions={0} | all-to-all | bytes 1310720 | tf_op jit(solution)/shard_map/all_to_all | solution.py:370
  83.5 6.6 %expert_fwd.1 = bf16[320,2048]{1,0:T(8,128)(2,1)} custom-call(bf16[320,1024]{1,0:T(8,128)(2,1)} %bitcast.38, bf16[192,768]{1,0:T(8,128)(2,1)} %get-tuple-element.13.right_hbm, bf16[2048,384]{1,0:T(8,128)(2,1)} %bitcast.47, bf16[2048,384]{1,0:T(8,128)(2,1)} %bitcast.49, bf16[384,2048]{1,0:T(8,128)(2,1)} %bitcast.51), custom_call_target="tpu_custom_call" | custom-call | flops 2516582400 | bytes 7340032 | tf_op jit(solution)/shard_map/expert_fwd/pallas_call | solution.py:481
  90.1 35.9 %all_to_all.17 = bf16[8,40,2048]{2,1,0:T(8,128)(2,1)} all-to-all(bf16[8,40,2048]{2,1,0:T(8,128)(2,1)} %bitcast.31), channel_id=1, replica_groups=mesh['dp'=16,'section'=8,'expert'=8] {'expert'}, dimensions={0} | all-to-all | bytes 2621440 | tf_op jit(solution)/shard_map/all_to_all | solution.py:370
  126.0 3.5 %combine.1 = (bf16[64,2048]{1,0:T(8,128)(2,1)}, bf16[64,2048]{1,0:T(8,128)(2,1)}) custom-call(bf16[320,2048]{1,0:T(8,128)(2,1)} %bitcast.27, s32[2,64]{1,0:T(2,128)} %bitcast.43, s32[2,64]{1,0:T(2,128)} %bitcast.41, f32[2,64]{1,0:T(2,128)} %bitcast.45, bf16[64,2048]{1,0:T(8,128)(2,1)} %bitcast.33, bf16[64,2048]{1,0:T(8,128)(2,1)} %bitcast.35, ...), custom_call_target="tpu_custom_call" | custom-call | flops 251658240 | bytes 2621440 | tf_op jit(solution)/shard_map/combine/pallas_call | solution.py:496
  129.5 0.0 collective-permute-start
  129.5 1.7 %collective-permute-start.1 = (bf16[64,2048]{1,0:T(8,128)(2,1)}, bf16[64,2048]{1,0:T(8,128)(2,1)}, u32[]{:S(2)}, u32[]{:S(2)}) collective-permute-start(bf16[64,2048]{1,0:T(8,128)(2,1)} %get-tuple-element.15), channel_id=1, source_target_pairs={{8,0},{16,8},{24,16},{32,24},{40,32},{48,40},{56,48},{0,56},{9,1},... | collective-permute-start | bytes 786440 | tf_op jit(solution)/shard_map/ppermute | solution.py:512
  131.2 4.4 %collective-permute-done.one_hbm = bf16[64,2048]{1,0:T(8,128)(2,1)} collective-permute-done((bf16[64,2048]{1,0:T(8,128)(2,1)}, bf16[64,2048]{1,0:T(8,128)(2,1)}, u32[]{:S(2)}, u32[]{:S(2)}) %collective-permute-start) | collective-permute-done | bytes 262176 | tf_op jit(solution)/shard_map/ppermute | solution.py:511
  135.6 0.0 collective-permute-done.1.two_hbm
  135.6 1.8 %settle.1 = (bf16[64,2048]{1,0:T(8,128)(2,1)}, bf16[64,2048]{1,0:T(8,128)(2,1)}) custom-call(bf16[64,2048]{1,0:T(8,128)(2,1)} %collective-permute-done.one_hbm, bf16[64,2048]{1,0:T(8,128)(2,1)} %collective-permute-done.1.two_hbm), custom_call_target="tpu_custom_call" | custom-call | bytes 1048576 | tf_op jit(solution)/shard_map/settle/pallas_call | solution.py:513
  137.4 10.5 %reduce-scatter.2.cloned.1.call-done.narrow_hbm = bf16[128,1152]{1,0:T(8,128)(2,1)} async-done(((bf16[2048,1152]{1,0:T(8,128)(2,1)}), bf16[128,1152]{1,0:T(8,128)(2,1)}) %reduce-scatter.2.cloned.1.call-update) | async-done | bytes 294928 | tf_op jit(solution)/shard_map/reduce_scatter | solution.py:462
  147.9 1.8 %widen.1 = f32[128,1152]{1,0:T(8,128)} custom-call(bf16[128,1152]{1,0:T(8,128)(2,1)} %reduce-scatter.2.cloned.1.call-done.narrow_hbm), custom_call_target="tpu_custom_call" | custom-call | bytes 884736 | tf_op jit(solution)/shard_map/widen/pallas_call | solution.py:463
Async XLA Ops:
  7.2 140.7 %reduce-scatter.2.cloned.1.call-start = ((), (), s32[]{:S(2)}) async-start(), calls=%async_computation.4 | async-start | bytes 5013504 | tf_op jit(solution)/shard_map/reduce_scatter | solution.py:462
  129.5 6.1 %collective-permute-start = (bf16[64,2048]{1,0:T(8,128)(2,1)}, bf16[64,2048]{1,0:T(8,128)(2,1)}, u32[]{:S(2)}, u32[]{:S(2)}) collective-permute-start(bf16[64,2048]{1,0:T(8,128)(2,1)} %get-tuple-element.14), channel_id=1, source_target_pairs={{0,8},{8,16},{16,24},{24,32},{32,40},{40,48},{48,56},{56,0},{1,9},... | collective-permute-start | bytes 786440 | tf_op jit(solution)/shard_map/ppermute | solution.py:511
  129.5 6.1 %collective-permute-start.1 = (bf16[64,2048]{1,0:T(8,128)(2,1)}, bf16[64,2048]{1,0:T(8,128)(2,1)}, u32[]{:S(2)}, u32[]{:S(2)}) collective-permute-start(bf16[64,2048]{1,0:T(8,128)(2,1)} %get-tuple-element.15), channel_id=1, source_target_pairs={{8,0},{16,8},{24,16},{32,24},{40,32},{48,40},{56,48},{0,56},{9,1},... | collective-permute-start | bytes 786440 | tf_op jit(solution)/shard_map/ppermute | solution.py:512
Sparse Core Ops, SparseCore 0:
  58.1 89.7 reduce-scatter.1
